TPU v7x, 128 devices: a whole 4x4x4 slice. The times are simulated.
128 devices in a mesh: blk: 8 (over y, core), expert: 16 (over x, z).
Axes of the slice: x: 4, y: 4, z: 4, core: 2. Of those that a mesh axis runs over, the one named last changes fastest.
Arguments:
- prefill_rows: bfloat16 [16384, 2048], P(('blk', 'expert')), may hold values from -6 to 6
- decode_rows: bfloat16 [4, 2048], replicated, may hold values from -6 to 6
- key_values: bfloat16 [2, 4, 16384, 2048], P(None, None, 'blk', 'expert')
- cache_length: int32 [4], replicated, may hold values from 1 to 16384, as said below
- attention_gain: float32 [2048], replicated, may hold values from 0.25 to 1.75
- feedforward_gain: float32 [2048], replicated, may hold values from 0.25 to 1.75
- query_key_value: bfloat16 [2048, 3, 2048], P(None, None, 'expert')
- out_projection: bfloat16 [2048, 2048], P('expert'), may hold values from -0.125 to 0.125
- routes: int32 [16384, 4], P(('blk', 'expert')), may hold values from 0 to 15, all different within a row; in each aligned block of 128 rows (0 to 127, 128 to 255, ...) at most 48 rows name the same one
- route_weight: float32 [16384, 4], P(('blk', 'expert')), may hold values from 0.1 to 0.6
- decode_routes: int32 [4, 4], replicated, may hold values from 0 to 15, as said below
- decode_weight: float32 [4, 4], replicated, may hold values from 0.5 to 1
- expert_gate_up: bfloat16 [16, 2048, 2816], P('expert'), may hold values from -0.125 to 0.125
- expert_down: bfloat16 [16, 1408, 2048], P('expert'), may hold values from -0.15625 to 0.15625
- shared_gate_up: bfloat16 [2048, 2, 5632], P(None, None, 'expert'), may hold values from -0.125 to 0.125
- shared_down: bfloat16 [5632, 2048], P('expert'), may hold values from -0.078125 to 0.078125
- shared_gate: float32 [2048], replicated, may hold values from -0.25 to 0.25
Outputs:
- prefill_out: bfloat16 [16384, 2048], P(('blk', 'expert'))
- decode_out: bfloat16 [4, 2048], replicated
Inputs may be any that keep to these rules, and one draw needn't show every extreme that they name: `routes`: each row names 4 different experts; among the rows of one device no expert is named more than 48 times, and some expert reaches that count. Request d's cache is valid at its first cache_length[d] positions; one request fills all 16384. `decode_routes`: each row names 4 different experts; every expert is named by some row.
All inputs are finite; a program needn't handle non-finite values.
Results may differ from a plain program's by a relative error of at most 0.02.
Values may be sent and summed in bfloat16 or wider, within the bound.
A program may use at most 128 MiB of HBM per device.

v0:
```python
import math

import jax
import jax.numpy as jnp
from jax import lax
from jax.sharding import PartitionSpec as P

HEAD_DIM = 128
REQUEST_LEN = 1024


eps_norm = 1e-06


def rms_normed(matrix, gain_vector):
    values = matrix.astype(jnp.float32)
    factor = lax.rsqrt(jnp.mean(values * values, axis=-1, keepdims=True) + eps_norm)
    return (values * factor * gain_vector).astype(jnp.bfloat16)


def gated_hidden(normed, gate_up):
    hidden = jnp.dot(normed, gate_up, preferred_element_type=jnp.float32)
    half_width = hidden.shape[1] // 2
    return (jax.nn.silu(hidden[:, :half_width]) * hidden[:, half_width:]).astype(jnp.bfloat16)


def prefill_attention(projected, local_heads):
    row_total = projected.shape[0]
    requests = row_total // REQUEST_LEN
    blocks = projected.reshape(requests, REQUEST_LEN, 3, local_heads, HEAD_DIM)
    position = jnp.arange(REQUEST_LEN)
    causal = position[:, None] >= position[None, :]
    score_scale = 1.0 / math.sqrt(HEAD_DIM)

    def one_request(request_block):
        scores = (
            jnp.einsum(
                "qhc,khc->hqk",
                request_block[:, 0],
                request_block[:, 1],
                preferred_element_type=jnp.float32,
            )
            * score_scale
        )
        scores = jnp.where(causal[None], scores, -jnp.inf)
        weights = jnp.exp(scores - jnp.max(scores, axis=-1, keepdims=True))
        probabilities = (weights / jnp.sum(weights, axis=-1, keepdims=True)).astype(jnp.bfloat16)
        mixture = jnp.einsum(
            "hqk,khc->qhc", probabilities, request_block[:, 2], preferred_element_type=jnp.float32
        )
        return mixture.astype(jnp.bfloat16)

    return lax.map(one_request, blocks).reshape(row_total, local_heads * HEAD_DIM)


def per_device(
    prefill_rows,
    decode_rows,
    key_values,
    cache_length,
    attention_gain,
    feedforward_gain,
    query_key_value,
    out_projection,
    routes,
    route_weight,
    decode_routes,
    decode_weight,
    expert_gate_up,
    expert_down,
    shared_gate_up,
    shared_down,
    shared_gate,
):
    expert_count = lax.axis_size("expert")
    local_rows = prefill_rows.shape[0]
    model_width = prefill_rows.shape[1]
    local_heads = out_projection.shape[0] // HEAD_DIM
    decode_count = decode_rows.shape[0]
    cache_span = key_values.shape[2]
    projection = query_key_value.reshape(model_width, 3 * local_heads * HEAD_DIM)
    shared_matrix = shared_gate_up.reshape(model_width, -1)
    score_scale = 1.0 / math.sqrt(HEAD_DIM)
    decode_normed = rms_normed(decode_rows, attention_gain)
    decode_projected = jnp.dot(
        decode_normed, projection, preferred_element_type=jnp.float32
    ).astype(jnp.bfloat16)
    decode_projected = decode_projected.reshape(decode_count, 3, local_heads, HEAD_DIM)
    query_rows = decode_projected[:, 0]
    cache_keys = key_values[0].reshape(decode_count, cache_span, local_heads, HEAD_DIM)
    cache_values = key_values[1].reshape(decode_count, cache_span, local_heads, HEAD_DIM)
    scores = (
        jnp.einsum("dhc,dphc->dhp", query_rows, cache_keys, preferred_element_type=jnp.float32)
        * score_scale
    )
    position = lax.axis_index("blk") * cache_span + jnp.arange(cache_span)
    valid = position[None, None, :] < cache_length[:, None, None]
    masked = jnp.where(valid, scores, -1e30)
    local_max = jnp.max(masked, axis=-1)
    weights = jnp.where(valid, jnp.exp(masked - local_max[:, :, None]), 0.0)
    local_sum = jnp.sum(weights, axis=-1)
    local_mix = jnp.einsum(
        "dhp,dphc->dhc", weights, cache_values.astype(jnp.float32), precision=lax.Precision.HIGHEST
    )
    global_max = lax.pmax(local_max, "blk")
    rescale = jnp.exp(local_max - global_max)
    total_sum, total_mix = lax.psum((local_sum * rescale, local_mix * rescale[:, :, None]), "blk")
    query_wide = query_rows.astype(jnp.float32)
    new_score = (
        jnp.sum(query_wide * decode_projected[:, 1].astype(jnp.float32), axis=-1) * score_scale
    )
    top_score = jnp.maximum(global_max, new_score)
    old_scale = jnp.exp(global_max - top_score)
    new_weight = jnp.exp(new_score - top_score)
    numerator = total_mix * old_scale[:, :, None] + new_weight[:, :, None] * decode_projected[
        :, 2
    ].astype(jnp.float32)
    denominator = total_sum * old_scale + new_weight
    decode_attended = (
        (numerator / denominator[:, :, None])
        .astype(jnp.bfloat16)
        .reshape(decode_count, local_heads * HEAD_DIM)
    )
    decode_term = jnp.dot(decode_attended, out_projection, preferred_element_type=jnp.float32)
    projected = jnp.dot(
        rms_normed(lax.all_gather(prefill_rows, "expert", axis=0, tiled=True), attention_gain),
        projection,
        preferred_element_type=jnp.float32,
    ).astype(jnp.bfloat16)
    attended = prefill_attention(projected, local_heads)
    head_sum = lax.psum_scatter(
        jnp.dot(attended, out_projection, preferred_element_type=jnp.float32).astype(jnp.bfloat16),
        "expert",
        scatter_dimension=0,
        tiled=True,
    ).astype(jnp.float32)
    decode_head = lax.psum(decode_term.astype(jnp.bfloat16), "expert").astype(jnp.float32)
    residual = (prefill_rows.astype(jnp.float32) + head_sum).astype(jnp.bfloat16)
    normed_two = rms_normed(residual, feedforward_gain)
    activated = gated_hidden(
        lax.all_gather(normed_two, "expert", axis=0, tiled=True), shared_matrix
    )
    shared_sum = lax.psum_scatter(
        jnp.dot(activated, shared_down, preferred_element_type=jnp.float32).astype(jnp.bfloat16),
        "expert",
        scatter_dimension=0,
        tiled=True,
    ).astype(jnp.float32)
    gate_value = jax.nn.sigmoid(jnp.sum(normed_two.astype(jnp.float32) * shared_gate, axis=-1))
    experts_total = expert_gate_up.shape[0] * expert_count
    choices_row = routes.shape[1]
    capacity = 3 * local_rows * choices_row // (2 * expert_count)
    flat_route = routes.reshape(-1)
    onehot = (flat_route[:, None] == jnp.arange(experts_total, dtype=jnp.int32)[None, :]).astype(
        jnp.int32
    )
    slot_index = jnp.sum((jnp.cumsum(onehot, axis=0) - 1) * onehot, axis=1)
    target = flat_route * capacity + slot_index
    source_row = jnp.arange(flat_route.shape[0]) // choices_row
    outgoing = (
        jnp.zeros((experts_total * capacity, model_width), jnp.bfloat16)
        .at[target]
        .set(normed_two[source_row])
    )
    outgoing = outgoing.reshape(experts_total, capacity, model_width)
    gate_up_local = expert_gate_up[0]
    down_local = expert_down[0]

    def expert_apply(received):
        flattened = received.reshape(-1, model_width)
        result = jnp.dot(
            gated_hidden(flattened, gate_up_local), down_local, preferred_element_type=jnp.float32
        )
        return result.astype(jnp.bfloat16).reshape(received.shape)

    processed = expert_apply(
        lax.all_to_all(outgoing, "expert", split_axis=0, concat_axis=0, tiled=True)
    )
    returned = lax.all_to_all(processed, "expert", split_axis=0, concat_axis=0, tiled=True)
    answers = returned.reshape(-1, model_width)[target].reshape(
        local_rows, choices_row, model_width
    )
    routed = jnp.sum(route_weight[:, :, None] * answers.astype(jnp.float32), axis=1)
    prefill_out = (residual.astype(jnp.float32) + gate_value[:, None] * shared_sum + routed).astype(
        jnp.bfloat16
    )
    decode_residual = (decode_rows.astype(jnp.float32) + decode_head).astype(jnp.bfloat16)
    decode_two = rms_normed(decode_residual, feedforward_gain)
    decode_part = jnp.dot(
        gated_hidden(decode_two, shared_matrix), shared_down, preferred_element_type=jnp.float32
    )
    decode_part = lax.optimization_barrier(decode_part.astype(jnp.bfloat16)).astype(jnp.float32)
    decode_expert = expert_apply(decode_two[None])[0]
    own_expert = lax.axis_index("expert")
    decode_scale = jnp.sum(jnp.where(decode_routes == own_expert, decode_weight, 0.0), axis=1)
    decode_shared, decode_routed = (
        lax.psum(decode_part.astype(jnp.bfloat16), "expert").astype(jnp.float32),
        lax.psum(
            (decode_scale[:, None] * decode_expert.astype(jnp.float32)).astype(jnp.bfloat16),
            "expert",
        ).astype(jnp.float32),
    )
    decode_gate = jax.nn.sigmoid(jnp.sum(decode_two.astype(jnp.float32) * shared_gate, axis=-1))
    decode_out = (
        decode_residual.astype(jnp.float32) + decode_gate[:, None] * decode_shared + decode_routed
    ).astype(jnp.bfloat16)
    return (prefill_out, decode_out)


def solution(mesh):
    return jax.shard_map(
        per_device,
        mesh=mesh,
        in_specs=(
            P(("blk", "expert"), None),
            P(),
            P(None, None, "blk", "expert"),
            P(),
            P(),
            P(),
            P(None, None, "expert"),
            P("expert", None),
            P(("blk", "expert"), None),
            P(("blk", "expert"), None),
            P(),
            P(),
            P("expert", None, None),
            P("expert", None, None),
            P(None, None, "expert"),
            P("expert", None),
            P(),
        ),
        out_specs=(P(("blk", "expert"), None), P()),
        check_vma=False,
    )
```

profile of v0, /device:TPU:0, one launch (start us, length us, event | category | flops | bytes accessed | tf_op | source)
XLA Modules:
  0.0 582.6 jit_solution(17154999694714717125)
XLA Ops:
  8.0 2.7 copy.30
  10.7 72.9 %all-gather.3.cloned.1.call-done = bf16[2048,2048]{1,0:T(8,128)(2,1)} async-done(((bf16[128,2048]{1,0:T(8,128)(2,1)}), bf16[2048,2048]{1,0:T(8,128)(2,1)}) %all-gather.3.cloned.1.call-update) | async-done | bytes 8388624 | tf_op jit(solution)/shard_map/all_gather | solution.py:126
  83.6 5.2 fusion.10
  89.4 7.1 %fusion.30 = bf16[2048,384]{1,0:T(8,128)(2,1)} fusion(bf16[2048,384]{0,1:T(8,128)(2,1)} %bitcast.157, bf16[2048,2048]{1,0:T(8,128)(2,1)S(1)} %copy-done.1, f32[2048]{0:T(1024)S(1)} %copy-done.9, f32[2048]{0:T(1024)S(1)} %add_rsqrt_fusion), kind=kOutput, calls=%fused_computation.45 | convolution fusion | flops 3238789120 | bytes 11550720 | tf_op jit(solution)/shard_map/dot_general | solution.py:125
  96.4 5.1 reshape.391
  101.6 3.0 copy.32
  104.5 8.2 %while.11 = (s32[]{:T(128)}, bf16[2,1024,1,128]{3,1,0,2:T(8,128)(2,1)}, bf16[2,1024,3,1,128]{4,1,3,2,0:T(8,128)(2,1)}, s32[]{:T(128)}) while((s32[]{:T(128)}, bf16[2,1024,1,128]{3,1,0,2:T(8,128)(2,1)}, bf16[2,1024,3,1,128]{4,1,3,2,0:T(8,128)(2,1)}, s32[]{:T(128)}) %tuple.37), condition=%wide.region_4.5_spmd.clone, body=%wide.region_1.4_spmd.clone.sunk | while | flops 552728576 | bytes 16273477 | solution.py:53
  112.7 6.8 %convolution_convert_fusion.1 = bf16[2048,2048]{1,0:T(8,128)(2,1)} fusion(bf16[2048,128]{1,0:T(8,128)(2,1)} %bitcast.160, bf16[128,2048]{1,0:T(8,128)(2,1)} %param.26), kind=kOutput, calls=%fused_computation.34 | convolution fusion | flops 1077936128 | bytes 9437184 | tf_op jit(solution)/shard_map/dot_general | solution.py:132
  119.5 85.5 %reduce-scatter.3.cloned.1.call-done = bf16[128,2048]{1,0:T(8,128)(2,1)} async-done(((bf16[2048,2048]{1,0:T(8,128)(2,1)}), bf16[128,2048]{1,0:T(8,128)(2,1)}) %reduce-scatter.3.cloned.1.call-update) | async-done | bytes 524304 | tf_op jit(solution)/shard_map/reduce_scatter | solution.py:131
  206.4 2.7 multiply_reduce_fusion.1
  209.6 69.8 %all-gather.5.cloned.1.call-done = bf16[2048,2048]{1,0:T(8,128)(2,1)} async-done(((bf16[128,2048]{1,0:T(8,128)(2,1)}), bf16[2048,2048]{1,0:T(8,128)(2,1)}) %all-gather.5.cloned.1.call-update) | async-done | bytes 8388624 | tf_op jit(solution)/shard_map/all_gather | solution.py:141
  279.4 8.7 %fusion.109 = f32[2048,704]{0,1:T(8,128)S(1)} fusion(bf16[2048,2048]{1,0:T(8,128)(2,1)} %all-gather.5.cloned.1.call-done, bf16[2048,704]{0,1:T(8,128)(2,1)S(1)} %bitcast.154), kind=kOutput, calls=%fused_computation.158 | convolution fusion | flops 5905580032 | bytes 17039360 | tf_op jit(solution)/shard_map/dot_general | solution.py:22
  288.1 6.9 %convolution_convert_fusion = bf16[2048,2048]{1,0:T(8,128)(2,1)} fusion(bf16[352,2048]{1,0:T(8,128)(2,1)S(1)} %copy-done.3, f32[2048,704]{0,1:T(8,128)S(1)} %fusion.109), kind=kOutput, calls=%fused_computation.33 | convolution fusion | flops 2961309696 | bytes 15597568 | tf_op jit(solution)/shard_map/dot_general | solution.py:144
  297.9 12.4 %scatter_custom_fusion = bf16[768,2048]{1,0:T(8,128)(2,1)} fusion(s32[512]{0:T(512)S(1)} %bitcast.162, bf16[128,2048]{1,0:T(8,128)(2,1)} %get-tuple-element.57, s32[1024]{0:T(1024)S(1)} %pad_clamp_fusion.1, bf16[]{:T(256)} %constant.42.clone.1), kind=kCustom, calls=%fused_computation.57 | custom fusion | bytes 3146240 | tf_op jit(solution)/shard_map/scatter | solution.py:163
  310.3 5.4 all-to-all-start
  315.8 1.9 fusion.58
  317.7 2.5 fusion.49
  320.4 14.9 %pmax.7 = f32[4,1]{0,1:T(1,128)S(1)} all-reduce(f32[4,1]{0,1:T(1,128)S(1)} %bitcast.166), channel_id=1, replica_groups=mesh['blk'=8,'expert'=16] {'blk'}, use_global_device_ids=true, to_apply=%region_16.17 | all-reduce | flops 4 | bytes 32 | tf_op jit(solution)/shard_map/pmax | solution.py:105
  335.6 2.5 fusion.47
  338.2 13.2 %all-reduce = (f32[4,1,128]{2,0,1:T(4,128)S(1)}, f32[4,1]{0,1:T(1,128)S(1)}) all-reduce(f32[4,1,128]{2,0,1:T(4,128)S(1)} %multiply_bitcast_fusion, f32[4,1]{0,1:T(1,128)S(1)} %get-tuple-element.63), channel_id=1, replica_groups=mesh['blk'=8,'expert'=16] {'blk'}, use_global_device_ids=true, to_apply=%region_17.18 | all-reduce | flops 516 | bytes 4128 | tf_op jit(solution)/shard_map/psum | solution.py:107
  352.8 78.0 %psum.37 = bf16[4,2048]{1,0:T(4,128)(2,1)S(1)} all-reduce(bf16[4,2048]{1,0:T(4,128)(2,1)S(1)} %convolution_convert_fusion.3), channel_id=1, replica_groups=mesh['blk'=8,'expert'=16] {'expert'}, use_global_device_ids=true, to_apply=%region_21.22 | all-reduce | flops 8192 | bytes 32768 | tf_op jit(solution)/shard_map/psum | solution.py:137
  430.9 13.7 %fusion.15 = f32[768,2816]{1,0:T(8,128)S(1)} fusion(bf16[768,2048]{1,0:T(8,128)(2,1)} %bitcast.8, bf16[1,2048,2816]{2,1,0:T(8,128)(2,1)} %param.31), kind=kOutput, calls=%fused_computation.28 | convolution fusion | flops 8858370048 | bytes 23330816 | tf_op jit(solution)/shard_map/dot_general | solution.py:22
  444.6 9.2 %fusion.26 = bf16[768,2048]{1,0:T(8,128)(2,1)} fusion(bf16[1,1408,2048]{2,1,0:T(8,128)(2,1)} %param.32, f32[768,2816]{1,0:T(8,128)S(1)} %fusion.15), kind=kOutput, calls=%fused_computation.42 | convolution fusion | flops 4437245952 | bytes 17563648 | tf_op jit(solution)/shard_map/dot_general | solution.py:171
  453.8 4.8 all-to-all-start.1
  460.2 1.7 convolution_convert_fusion.2
  462.1 5.9 %fusion.13 = f32[4,2816]{1,0:T(4,128)S(1)} fusion(bf16[4,2048]{1,0:T(4,128)(2,1)S(1)} %get-tuple-element.53, bf16[1,2048,2816]{2,1,0:T(8,128)(2,1)} %param.31), kind=kOutput, calls=%fused_computation.26 | convolution fusion | flops 46137344 | bytes 11595776 | tf_op jit(solution)/shard_map/dot_general | solution.py:22
  467.9 3.5 fusion.42
  471.4 79.6 %all-reduce.1 = (bf16[4,2048]{1,0:T(4,128)(2,1)S(1)}, bf16[4,2048]{1,0:T(4,128)(2,1)}) all-reduce(bf16[4,2048]{1,0:T(4,128)(2,1)S(1)} %fusion.42, bf16[4,2048]{1,0:T(4,128)(2,1)S(1)} %convolution_convert_fusion.2), channel_id=1, replica_groups=mesh['blk'=8,'expert'=16] {'expert'}, use_global_device_ids=true, to_apply=%region_26.27 | all-reduce | flops 16384 | bytes 65536 | tf_op jit(solution)/shard_map/psum | solution.py:198
  554.5 7.5 %gather_fusion = bf16[512,2048]{1,0:T(8,128)(2,1)} fusion(bf16[768,2048]{1,0:T(8,128)(2,1)} %bitcast.12, s32[1024]{0:T(1024)S(1)} %pad_clamp_fusion), kind=kCustom, calls=%fused_computation.1 | custom fusion | bytes 4196352 | tf_op jit(solution)/shard_map/gather | solution.py:180
  562.0 4.8 reshape.358
  566.8 6.4 %multiply_reduce_fusion = f32[128,2048]{1,0:T(8,128)} fusion(f32[128,4,2048]{2,1,0:T(4,128)} %reshape.358, f32[128,4]{1,0:T(8,128)S(1)} %copy.34), kind=kLoop, calls=%fused_computation.41 | loop fusion | flops 1835008 | bytes 5244928 | tf_op jit(solution)/shard_map/reduce_sum | solution.py:183
  573.2 2.6 fusion.63
  (95 shorter events, 21.5 us)
Async XLA Ops:
  7.2 272.2 %copy-start = (bf16[2048,2,352]{0,2,1:T(8,128)(2,1)S(1)}, bf16[2048,2,352]{0,2,1:T(8,128)(2,1)}, u32[]{:S(2)}) copy-start(bf16[2048,2,352]{0,2,1:T(8,128)(2,1)} %param.33) | copy-start | bytes 8650756
  7.2 76.4 %all-gather.3.cloned.1.call-start = ((), (), s32[]{:S(2)}) async-start(), calls=%async_computation.4 | async-start | bytes 8912896 | tf_op jit(solution)/shard_map/all_gather | solution.py:126
  7.9 197.1 %reduce-scatter.3.cloned.1.call-start = ((), (), s32[]{:S(2)}) async-start(), calls=%async_computation.5 | async-start | bytes 8912896 | tf_op jit(solution)/shard_map/reduce_scatter | solution.py:131
  10.7 78.2 %copy-start.9 = (f32[2048]{0:T(1024)S(1)}, f32[2048]{0:T(1024)}, u32[]{:S(2)}) copy-start(f32[2048]{0:T(1024)} %param.23) | copy-start | bytes 24580
  83.6 5.8 copy-start.1
  119.5 85.6 %copy-start.2 = (bf16[128,2048]{1,0:T(8,128)(2,1)S(1)}, bf16[128,2048]{1,0:T(8,128)(2,1)}, u32[]{:S(2)}) copy-start(bf16[128,2048]{1,0:T(8,128)(2,1)} %param.19) | copy-start | bytes 1572868
  119.5 86.9 %copy-start.5 = (f32[2048]{0:T(1024)S(1)}, f32[2048]{0:T(1024)}, u32[]{:S(2)}) copy-start(f32[2048]{0:T(1024)} %param.35) | copy-start | bytes 24580
  119.5 86.9 %copy-start.7 = (f32[2048]{0:T(1024)S(1)}, f32[2048]{0:T(1024)}, u32[]{:S(2)}) copy-start(f32[2048]{0:T(1024)} %param.24) | copy-start | bytes 24580
  119.5 159.9 %all-gather.5.cloned.1.call-start = ((), (), s32[]{:S(2)}) async-start(), calls=%async_computation.6 | async-start | bytes 8912896 | tf_op jit(solution)/shard_map/all_gather | solution.py:141
  209.1 364.1 %reduce-scatter.5.cloned.1.call-start = ((), (), s32[]{:S(2)}) async-start(), calls=%async_computation.7 | async-start | bytes 8912896 | tf_op jit(solution)/shard_map/reduce_scatter | solution.py:143
  279.4 8.7 %copy-start.3 = (bf16[352,2048]{1,0:T(8,128)(2,1)S(1)}, bf16[352,2048]{1,0:T(8,128)(2,1)}, u32[]{:S(2)}) copy-start(bf16[352,2048]{1,0:T(8,128)(2,1)} %param.34) | copy-start | bytes 4325380
  295.0 0.7 copy-start.11
  295.0 2.7 copy-start.4
  297.9 12.4 %copy-start.10 = (s32[512,1]{0,1:T(1,128)}, s32[512,1]{0,1:T(1,128)S(1)}, u32[]{:S(2)}) copy-start(s32[512,1]{0,1:T(1,128)S(1)} %compare_select_fusion.3) | copy-start | bytes 6148
  310.3 9.9 %copy-start.12 = (s32[4]{0:T(128)S(1)}, s32[4]{0:T(128)}, u32[]{:S(2)}) copy-start(s32[4]{0:T(128)} %param.22) | copy-start | bytes 52
  310.3 25.0 %copy-start.13 = (f32[128,4]{0,1:T(4,128)S(1)}, f32[128,4]{0,1:T(4,128)}, u32[]{:S(2)}) copy-start(f32[128,4]{0,1:T(4,128)} %param.28) | copy-start | bytes 6148
  310.3 120.6 %all-to-all-start = ((bf16[16,48,2048]{2,1,0:T(8,128)(2,1)}), bf16[16,48,2048]{2,1,0:T(8,128)(2,1)}, u32[]{:S(2)}, u32[]{:S(2)}) async-start(bf16[16,48,2048]{2,1,0:T(8,128)(2,1)} %bitcast.156), calls=%async_computation.2 | async-start | bytes 6291456 | tf_op jit(solution)/shard_map/all_to_all | solution.py:177
  453.8 4.9 copy-start.6
  453.8 4.9 copy-start.8
  453.8 8.1 %copy-start.14 = (f32[4,4]{1,0:T(4,128)S(1)}, f32[4,4]{1,0:T(4,128)}, u32[]{:S(2)}) copy-start(f32[4,4]{1,0:T(4,128)} %param.30) | copy-start | bytes 196
  453.8 100.7 %all-to-all-start.1 = ((bf16[16,48,2048]{2,1,0:T(8,128)(2,1)}), bf16[16,48,2048]{2,1,0:T(8,128)(2,1)}, u32[]{:S(2)}, u32[]{:S(2)}) async-start(bf16[16,48,2048]{2,1,0:T(8,128)(2,1)} %bitcast.159), calls=%async_computation.3 | async-start | bytes 6291456 | tf_op jit(solution)/shard_map/all_to_all | solution.py:179
  458.7 3.3 copy-start.15
Sparse Core Ops, SparseCore 0:
  10.1 73.4 all-gather.2
  119.6 85.3 reduce-scatter.2
  209.2 70.1 all-gather.4
  295.1 120.4 reduce-scatter.4
where the time goes:
time: 591 us; the launch traced here: 583 us
  waiting for transfers between devices  229 us (39%)
  blocking collectives  186 us (31%)
  matrix products  75.3 us (13%)
  local copies, waits for them, and re-layouts  41.8 us (7%)
  other arithmetic  25.8 us (4%)
  between operations  14.2 us (2%)
  starting transfers between devices  10.9 us (2%)
    reduce_scatter x1, waiting for transfers between devices, per_device(): lax.psum_scatter(jnp.dot(attended, out_projection, preferred_element_type...  85.5 us
    psum x1, blocking collectives, per_device(): lax.psum((decode_scale[:, None] * decode_expert.astype(jnp.float32)).asty...  79.6 us
    psum x1, blocking collectives, per_device(): lax.psum(decode_term.astype(jnp.bfloat16), 'expert').astype(jnp.float32)  78 us
    all_gather x1, waiting for transfers between devices, per_device(): lax.all_gather(prefill_rows, 'expert', axis=0, tiled=True)  72.9 us
    all_gather x1, waiting for transfers between devices, per_device(): lax.all_gather(normed_two, 'expert', axis=0, tiled=True)  69.8 us
    dot_general x4, matrix products, gated_hidden(): hidden = jnp.dot(normed, gate_up, preferred_element_type=jnp.float32)  29.1 us
    pmax x1, blocking collectives, per_device(): global_max = lax.pmax(local_max, 'blk')  14.9 us
    psum x1, blocking collectives, per_device(): lax.psum((local_sum * rescale, local_mix * rescale[:, :, None]), 'blk')  13.2 us
  transfers between devices with their start and end apart: 6, of which 3 were waited for; matrix products, arithmetic and copies ran while one was open for 14% of the time, Pallas kernels for 0%

commit v1 on v0

v1 whole, which is shorter than its diff:
```python
import math

import jax
import jax.numpy as jnp
from jax import lax
from jax.experimental import pallas as pl
from jax.experimental.pallas import tpu as pltpu
from jax.sharding import PartitionSpec as P

HEAD_DIM = 128
REQUEST_LEN = 1024
EPS = 1e-06
MESH = pl.DeviceIdType.MESH
F32 = jnp.float32
BF16 = jnp.bfloat16

BATCHES = (
    ((0, 0), (0, 1), (0, 3), (1, 0), (3, 0)),
    ((1, 1), (1, 3), (3, 1), (3, 3), (2, 0), (0, 2)),
    ((1, 2), (3, 2), (2, 1), (2, 3), (2, 2)),
)
SLOT = {place: at for at, place in enumerate(sum(BATCHES, ()))}
STARTS = (0, 5, 11)


def nn(a, b):
    return lax.dot_general(a, b, (((1,), (0,)), ((), ())), preferred_element_type=F32)


def nt(a, b):
    return lax.dot_general(a, b, (((1,), (1,)), ((), ())), preferred_element_type=F32)


def normed(values, gain):
    factor = lax.rsqrt(jnp.mean(values * values, axis=-1, keepdims=True) + EPS)
    return (values * factor * gain).astype(BF16)


def silu(v):
    return v * (1.0 / (1.0 + jnp.exp(-v)))


class Place:
    def __init__(self):
        self.b = lax.axis_index("blk")
        self.e = lax.axis_index("expert")
        self.x = self.e // 4
        self.z = self.e % 4

    def at(self, dx, dz):
        return (self.b, ((self.x + dx) % 4) * 4 + (self.z + dz) % 4)

    def block(self, place):
        return ((self.x + place[0]) % 4) * 4 + (self.z + place[1]) % 4


def greet(peers):
    barrier = pltpu.get_barrier_semaphore()
    for peer in peers:
        pl.semaphore_signal(barrier, inc=1, device_id=peer, device_id_type=MESH)
    return lambda: pl.semaphore_wait(barrier, len(peers))


def remote(src, dst, send, recv, at, device):
    return pltpu.make_async_remote_copy(
        src_ref=src,
        dst_ref=dst,
        send_sem=send.at[at],
        recv_sem=recv.at[at],
        device_id=device,
        device_id_type=MESH,
    )


def slot(half, p, q):
    return SLOT[(p, q) if half == 0 else (q, p)]


def sides(here, half):
    along_x = (here.at(1, 0), here.at(3, 0))
    along_z = (here.at(0, 1), here.at(0, 3))
    return along_x + along_z if half == 0 else along_z + along_x


class Gather:
    def __init__(self, here, rows_ref, rows, send, recv, base):
        self.copies = []
        hr = rows // 2
        for half in range(2):
            major_p, major_m, minor_p, minor_m = sides(here, half)
            c = {}

            def put(name, at, src, dst, part, device):
                lo, size = part
                c[name] = remote(
                    rows_ref.at[half, pl.ds(slot(half, *src) * rows + lo, size)],
                    rows_ref.at[half, pl.ds(slot(half, *dst) * rows + lo, size)],
                    send,
                    recv,
                    base + half * 20 + at,
                    device,
                )

            whole, low, high = (0, rows), (0, hr), (hr, hr)
            put("n+", 0, (0, 0), (0, 3), whole, minor_p)
            put("n-", 1, (0, 0), (0, 1), whole, minor_m)
            put("fn+", 4, (0, 3), (0, 2), high, minor_p)
            put("fn-", 5, (0, 1), (0, 2), low, minor_m)
            for q, at in ((0, 2), (1, 6), (3, 8), (2, 10)):
                put(("j+", q), at, (0, q), (3, q), whole, major_p)
                put(("j-", q), at + 1, (0, q), (1, q), whole, major_m)
            for q, at in ((0, 12), (1, 14), (3, 16), (2, 18)):
                put(("f+", q), at, (3, q), (2, q), high, major_p)
                put(("f-", q), at + 1, (1, q), (2, q), low, major_m)
            self.copies.append(c)

    def start(self, *names):
        for c in self.copies:
            for name in names:
                c[name].start()

    def got(self, *names):
        for c in self.copies:
            for name in names:
                c[name].wait_recv()

    def open(self):
        self.start("n+", "n-", ("j+", 0), ("j-", 0))

    def to_batch_0(self):
        self.got("n+", "n-")
        self.start("fn+", "fn-", ("j+", 1), ("j-", 1), ("j+", 3), ("j-", 3))
        self.got(("j+", 0), ("j-", 0))
        self.start(("f+", 0), ("f-", 0))

    def to_batch_1(self):
        self.got("fn+", "fn-")
        self.start(("j+", 2), ("j-", 2))
        self.got(("j+", 1), ("j-", 1))
        self.start(("f+", 1), ("f-", 1))
        self.got(("j+", 3), ("j-", 3))
        self.start(("f+", 3), ("f-", 3))
        self.got(("f+", 0), ("f-", 0))

    def to_batch_2(self):
        self.got(("j+", 2), ("j-", 2))
        self.start(("f+", 2), ("f-", 2))
        for q in (1, 3, 2):
            self.got(("f+", q), ("f-", q))

    def close(self):
        for c in self.copies:
            for copy in c.values():
                copy.wait_send()


class Scatter:
    def __init__(self, here, part_ref, fwd_ref, full_ref, send, recv, base):
        self.part, self.fwd, self.full = part_ref, fwd_ref, full_ref
        self.copies = []
        rows = part_ref.shape[2]
        hr = rows // 2
        self.low, self.high = pl.ds(0, hr), pl.ds(hr, hr)
        for half in range(2):
            major_p, major_m, minor_p, minor_m = sides(here, half)
            c = {}

            def put(q, far, plus, minus, side_p, side_m):
                at = base + half * 20 + 4 * q
                c["f+", q] = remote(
                    part_ref.at[half, far, self.low], fwd_ref.at[half, q, 0], send, recv, at, side_p
                )
                c["f-", q] = remote(
                    part_ref.at[half, far, self.high], fwd_ref.at[half, q, 1], send, recv, at + 1, side_m
                )
                c["t+", q] = remote(
                    part_ref.at[half, plus], full_ref.at[half, q, 0], send, recv, at + 2, side_p
                )
                c["t-", q] = remote(
                    part_ref.at[half, minus], full_ref.at[half, q, 1], send, recv, at + 3, side_m
                )

            for q in range(4):
                put(q, slot(half, 2, q), slot(half, 1, q), slot(half, 3, q), major_p, major_m)
            put(4, slot(half, 0, 2), slot(half, 0, 1), slot(half, 0, 3), minor_p, minor_m)
            self.copies.append(c)

    def _next(self, half, q, p):
        return slot(half, p, q) if q < 4 else slot(half, 0, p)

    def send_far(self, *qs):
        for q in qs:
            for half in range(2):
                self.copies[half]["f+", q].start()
                self.copies[half]["f-", q].start()

    def pass_plus(self, half, q):
        c = self.copies[half]
        c["f+", q].wait_recv()
        at = self._next(half, q, 1)
        self.part[half, at, self.low] = (
            self.part[half, at, self.low].astype(F32) + self.fwd[half, q, 0].astype(F32)
        ).astype(BF16)
        c["t+", q].start()

    def pass_minus(self, half, q):
        c = self.copies[half]
        c["f-", q].wait_recv()
        at = self._next(half, q, 3)
        self.part[half, at, self.high] = (
            self.part[half, at, self.high].astype(F32) + self.fwd[half, q, 1].astype(F32)
        ).astype(BF16)
        c["t-", q].start()

    def pass_on(self, *qs):
        for q in qs:
            for half in range(2):
                self.pass_plus(half, q)
                self.pass_minus(half, q)

    def total(self, half, q):
        c = self.copies[half]
        c["t+", q].wait_recv()
        c["t-", q].wait_recv()
        at = self._next(half, q, 0)
        return (
            self.part[half, at].astype(F32)
            + self.full[half, q, 0].astype(F32)
            + self.full[half, q, 1].astype(F32)
        )

    def line(self, q):
        for half in range(2):
            self.part[half, slot(half, 0, q)] = self.total(half, q).astype(BF16)

    def finish(self):
        self.line(2)
        self.send_far(4)
        self.line(1)
        for half in range(2):
            self.pass_plus(half, 4)
        self.line(3)
        for half in range(2):
            self.pass_minus(half, 4)
        self.line(0)
        return [self.total(half, 4) for half in range(2)]

    def close(self):
        for c in self.copies:
            for copy in c.values():
                copy.wait_send()


def padded_rows(ref, scratch):
    scratch[...] = jnp.zeros_like(scratch)
    scratch[0 : ref.shape[0], :] = ref[...].astype(F32)
    return scratch[...]


def attention_kernel(
    rows_ref,
    dec_ref,
    cache_hbm,
    length_ref,
    gain_ref,
    qkv_hbm,
    att_ref,
    dec_att_ref,
    g,
    wqkv,
    cache,
    heads,
    dec8,
    dec_out,
    dec_in,
    send,
    recv,
    local_sem,
):
    here = Place()
    rows, width = rows_ref.shape
    hw = width // 2
    blk_count = lax.axis_size("blk")
    score_scale = 1.0 / math.sqrt(HEAD_DIM)
    w_copy = pltpu.make_async_copy(qkv_hbm, wqkv, local_sem.at[0])
    c_copy = pltpu.make_async_copy(cache_hbm, cache, local_sem.at[1])
    w_copy.start()
    c_copy.start()
    core, y = here.b % 2, here.b // 2
    blk_peers = []
    if blk_count > 1:
        blk_peers = [(here.b + 1 - 2 * core, here.e)]
        blk_peers += [(((y + k) % 4) * 2 + core, here.e) for k in (1, 3, 2)]
    wait_all = greet([here.at(1, 0), here.at(3, 0), here.at(0, 1), here.at(0, 3)] + blk_peers)
    own = normed(rows_ref[...].astype(F32), gain_ref[...])
    g[0, 0:rows] = own[:, :hw]
    g[1, 0:rows] = own[:, hw:]
    wait_all()
    gather = Gather(here, g, rows, send, recv, 0)
    gather.open()

    dn = normed(padded_rows(dec_ref, dec8), gain_ref[...])
    w_copy.wait()
    q8 = nn(dn, wqkv[0]).astype(BF16)
    k8 = nn(dn, wqkv[1]).astype(BF16)
    v8 = nn(dn, wqkv[2]).astype(BF16)
    c_copy.wait()
    count = cache.shape[1]
    span = cache.shape[2]
    row = lax.broadcasted_iota(jnp.int32, (8, 1), 0)
    scores = jnp.zeros((8, span), F32)
    lengths = jnp.zeros((8, 1), jnp.int32)
    for d in range(count):
        scores = jnp.where(row == d, nt(q8, cache[0, d]), scores)
        lengths = jnp.where(row == d, length_ref[d], lengths)
    position = here.b * span + lax.broadcasted_iota(jnp.int32, (8, span), 1)
    valid = position < lengths
    masked = jnp.where(valid, scores * score_scale, -1e30)
    top = jnp.max(masked, axis=-1, keepdims=True)
    weights = jnp.where(valid, jnp.exp(masked - top), 0.0)
    total = jnp.sum(weights, axis=-1, keepdims=True)
    coarse = weights.astype(BF16).astype(F32)
    both = jnp.concatenate([coarse, weights - coarse], axis=0).astype(BF16)
    mix = jnp.zeros((8, HEAD_DIM), F32)
    for d in range(count):
        pair = nn(both, cache[1, d])
        mix = jnp.where(row == d, pair[0:8] + pair[8:16], mix)

    def pack(at, mix, top, total):
        dec_out[at, 0:8] = mix
        dec_out[at, 8:16] = jnp.broadcast_to(top, (8, HEAD_DIM))
        dec_out[at, 16:24] = jnp.broadcast_to(total, (8, HEAD_DIM))

    def merge(mix, top, total, at):
        other_top = dec_in[at, 8:16]
        new_top = jnp.maximum(top, other_top)
        mine, theirs = jnp.exp(top - new_top), jnp.exp(other_top - new_top)
        return (
            mix * mine + dec_in[at, 0:8] * theirs,
            new_top,
            total * mine + dec_in[at, 16:24] * theirs,
        )

    top = jnp.broadcast_to(top, (8, HEAD_DIM))
    total = jnp.broadcast_to(total, (8, HEAD_DIM))
    pack(0, mix, top, total)
    blk_copies = [
        remote(dec_out.at[min(k, 1)], dec_in.at[k], send, recv, 40 + k, peer)
        for k, peer in enumerate(blk_peers)
    ]
    for copy in blk_copies[:1]:
        copy.start()

    q_s, k_s, v_s = heads.at[0], heads.at[1], heads.at[2]

    def project(batch):
        lo, size = STARTS[batch] * rows, len(BATCHES[batch]) * rows
        left, right = g[0, lo : lo + size], g[1, lo : lo + size]
        for which, ref in enumerate((q_s, k_s, v_s)):
            out = (nn(left, wqkv[which, 0:hw]) + nn(right, wqkv[which, hw:width])).astype(BF16)
            for j, place in enumerate(BATCHES[batch]):
                at = pl.multiple_of(here.block(place) * rows, rows)
                ref[pl.ds(at, rows)] = out[j * rows : (j + 1) * rows]

    gather.to_batch_0()
    project(0)
    gather.to_batch_1()
    if blk_copies:
        blk_copies[0].wait_recv()
        mix, top, total = merge(mix, top, total, 0)
        pack(1, mix, top, total)
        for copy in blk_copies[1:]:
            copy.start()
    project(1)
    gather.to_batch_2()
    project(2)
    for k, copy in enumerate(blk_copies[1:]):
        copy.wait_recv()
        mix, top, total = merge(mix, top, total, k + 1)
    q32, k32, v32 = q8.astype(F32), k8.astype(F32), v8.astype(F32)
    new_score = jnp.sum(q32 * k32, axis=-1, keepdims=True) * score_scale
    new_top = jnp.maximum(top, new_score)
    old = jnp.exp(top - new_top)
    fresh = jnp.exp(new_score - new_top)
    dec_att_ref[...] = ((mix * old + fresh * v32) / (total * old + fresh)).astype(BF16)

    step = 256
    diagonal = lax.broadcasted_iota(jnp.int32, (step, step), 0) >= lax.broadcasted_iota(
        jnp.int32, (step, step), 1
    )

    def one_request(r, carry):
        first = pl.multiple_of(r * REQUEST_LEN, REQUEST_LEN)
        for qb in range(REQUEST_LEN // step):
            at = pl.multiple_of(first + qb * step, step)
            q = q_s[pl.ds(at, step)]
            s1 = jnp.where(diagonal, nt(q, k_s[pl.ds(at, step)]) * score_scale, -jnp.inf)
            top_q = jnp.max(s1, axis=-1, keepdims=True)
            if qb:
                s0 = nt(q, k_s[pl.ds(first, qb * step)]) * score_scale
                top_q = jnp.maximum(top_q, jnp.max(s0, axis=-1, keepdims=True))
            p1 = jnp.exp(s1 - top_q)
            sum_q = jnp.sum(p1, axis=-1, keepdims=True)
            out = nn(p1.astype(BF16), v_s[pl.ds(at, step)])
            if qb:
                p0 = jnp.exp(s0 - top_q)
                sum_q = sum_q + jnp.sum(p0, axis=-1, keepdims=True)
                out = out + nn(p0.astype(BF16), v_s[pl.ds(first, qb * step)])
            att_ref[pl.ds(at, step)] = (out / sum_q).astype(BF16)
        return carry

    lax.fori_loop(0, att_ref.shape[0] // REQUEST_LEN, one_request, 0)
    gather.close()
    for copy in blk_copies:
        copy.wait_send()


def layer_kernel(
    rows_ref,
    dec_ref,
    att_ref,
    dec_att_ref,
    gain_ref,
    wo_ref,
    routes_ref,
    weight_ref,
    dec_routes_ref,
    dec_weight_ref,
    gate_ref,
    wgu_hbm,
    wd_hbm,
    wst_hbm,
    wsd_hbm,
    out_ref,
    dec_out_ref,
    g,
    part,
    fwd,
    full,
    wgu,
    wd,
    wsp,
    wsd,
    xe,
    he,
    ye,
    hs,
    gv,
    wslot,
    pick,
    back,
    meta,
    dec8,
    dec_send,
    dec_recv,
    res,
    send,
    recv,
    local_sem,
):
    here = Place()
    rows, width = rows_ref.shape
    hw = width // 2
    cap = pick.shape[1]
    ff = wd.shape[0]
    sff = wsd_hbm.shape[0]
    count = dec_ref.shape[0]
    tail = sff - 256
    tile = min(256, hw)

    moves = [(wgu_hbm, wgu), (wd_hbm, wd), (wsd_hbm, wsd.at[pl.ds(0, sff)])]
    for group, size in enumerate((128, 128, tail)):
        for kind in range(2):
            moves.append(
                (
                    wst_hbm.at[kind, pl.ds(group * 128, size)],
                    wsp.at[pl.ds(group * 256 + kind * 128, size)],
                )
            )
    local = [pltpu.make_async_copy(a, b, local_sem.at[i]) for i, (a, b) in enumerate(moves)]
    for copy in local:
        copy.start()
    peers = [here.at(1, 0), here.at(3, 0), here.at(0, 1), here.at(0, 3), here.at(2, 0), here.at(0, 2)]
    wait_all = greet(peers)

    weight = weight_ref[...]
    coarse = weight.astype(BF16).astype(F32)
    meta[0, 0] = jnp.concatenate(
        [routes_ref[...].astype(F32), coarse, weight - coarse, jnp.zeros_like(weight)], axis=0
    ).astype(BF16)

    def out_project(*places):
        for place in places:
            at = pl.multiple_of(here.block(place) * rows, rows)
            term = nn(att_ref[pl.ds(at, rows)], wo_ref[...]).astype(BF16)
            part[0, SLOT[place]] = term[:, :hw]
            part[1, SLOT[place]] = term[:, hw:]

    first = Scatter(here, part, fwd, full, send, recv, 0)
    gather = Gather(here, g, rows, send, recv, 40)
    second = Scatter(here, part, fwd, full, send, recv, 80)

    def exchange(buf_send, buf_recv, base, along):
        steps = ((1, 0), (3, 0), (2, 0)) if along == 0 else ((0, 1), (0, 3), (0, 2))
        return [
            remote(buf_send, buf_recv.at[k], send, recv, base + k, here.at(*step))
            for k, step in enumerate(steps)
        ]

    meta_z = [
        remote(meta.at[0, 0], meta.at[0, dst], send, recv, 120 + k, here.at(0, dz))
        for k, (dz, dst) in enumerate(((1, 3), (3, 1), (2, 2)))
    ]
    meta_x = [
        remote(meta.at[0], meta.at[dst], send, recv, 123 + k, here.at(dx, 0))
        for k, (dx, dst) in enumerate(((1, 3), (3, 1), (2, 2)))
    ]
    dec_copies = [
        exchange(dec_send.at[k], dec_recv.at[k], 126 + 3 * k, 1 - k % 2) for k in range(4)
    ]

    out_project((2, 2))
    dec_term = nn(dec_att_ref[...], wo_ref[...])
    dec_send[0] = dec_term.astype(BF16)
    wait_all()
    first.send_far(2)
    for copy in meta_z + dec_copies[0]:
        copy.start()
    out_project((2, 1), (1, 2))
    first.send_far(1)
    out_project((2, 3), (3, 2))
    first.send_far(3)
    out_project((2, 0), (0, 2))
    first.send_far(0)
    out_project((1, 1), (3, 1), (1, 3), (3, 3))
    first.pass_on(2)
    out_project((1, 0), (3, 0), (0, 1), (0, 3), (0, 0))
    first.pass_on(1)

    def dec_sum(k):
        total = dec_send[k].astype(F32)
        for copy in dec_copies[k]:
            copy.wait_recv()
        for at in range(3):
            total = total + dec_recv[k, at].astype(F32)
        return total

    for copy in meta_z:
        copy.wait_recv()
    for copy in meta_x:
        copy.start()
    dec_send[1] = dec_sum(0).astype(BF16)
    for copy in dec_copies[1]:
        copy.start()
    first.pass_on(3, 0)

    gate = gate_ref[...]
    gate_coarse = gate.astype(BF16).astype(F32)
    for copy in local:
        copy.wait()
    pad = 128 - tail
    row_at = lax.broadcasted_iota(jnp.int32, (pad, width), 0)
    wsp[512 + tail : 640] = jnp.where(
        row_at == 0, gate_coarse, jnp.where(row_at == 1, gate - gate_coarse, 0.0)
    ).astype(BF16)
    wsp[640 + tail : 768] = jnp.zeros((pad, width), BF16)
    wsd[sff : wsd.shape[0]] = jnp.zeros((wsd.shape[0] - sff, width), BF16)

    for copy in meta_x:
        copy.wait_recv()
    expert = here.e.astype(F32)
    iota_r = lax.broadcasted_iota(jnp.int32, (rows, rows), 0)
    iota_c = lax.broadcasted_iota(jnp.int32, (rows, rows), 1)
    upper = (iota_r <= iota_c).astype(F32).astype(BF16)
    eye = (iota_r == iota_c).astype(F32).astype(BF16)
    iota_cap = lax.broadcasted_iota(jnp.int32, (cap, rows), 0).astype(F32)
    iota_lane = iota_c.astype(F32)
    for place, at in SLOT.items():
        info = meta[place[0], place[1]].astype(F32)
        match = info[0:4] == expert
        chosen = jnp.sum(match.astype(F32), axis=0, keepdims=True)
        scale = jnp.sum(jnp.where(match, info[4:8] + info[8:12], 0.0), axis=0, keepdims=True)
        order = nn(jnp.broadcast_to(chosen, (8, rows)).astype(BF16), upper)[0:1] - 1.0
        order = jnp.where(chosen > 0.0, order, -1.0)
        choice = iota_cap == order
        pick[at] = choice.astype(F32).astype(BF16)
        wslot[at] = jnp.broadcast_to(
            jnp.sum(jnp.where(choice, scale, 0.0), axis=1, keepdims=True), (cap, 128)
        )
        column = nt(eye, jnp.broadcast_to(order, (8, rows)).astype(BF16))[:, 0:1]
        back[at] = (iota_lane == column).astype(F32).astype(BF16)

    dec_res = (padded_rows(dec_ref, dec8) + dec_sum(1)).astype(BF16).astype(F32)
    dec_two = normed(dec_res, gain_ref[...])
    dec8[...] = dec_res
    base_row = 16 * rows
    dec_pad = jnp.concatenate([dec_two.astype(F32), jnp.zeros((8, width), F32)], axis=0).astype(BF16)
    g[0, base_row : base_row + 16] = dec_pad[:, :hw]
    g[1, base_row : base_row + 16] = dec_pad[:, hw:]

    halves = first.finish()
    sum_sq = jnp.zeros((rows, 1), F32)
    for half in range(2):
        cols = pl.ds(half * hw, hw)
        value = (rows_ref[:, cols].astype(F32) + halves[half]).astype(BF16)
        res[:, cols] = value
        wide = value.astype(F32)
        sum_sq = sum_sq + jnp.sum(wide * wide, axis=-1, keepdims=True)
    factor = lax.rsqrt(sum_sq / width + EPS)
    for half in range(2):
        cols = pl.ds(half * hw, hw)
        g[half, 0:rows] = (res[:, cols].astype(F32) * factor * gain_ref[:, cols]).astype(BF16)
    gather.open()
    first.close()

    row8 = lax.broadcasted_iota(jnp.int32, (16, 1), 0)
    dec_scale = jnp.zeros((16, 1), F32)
    for d in range(count):
        one = jnp.float32(0.0)
        for k in range(dec_routes_ref.shape[1]):
            one = one + jnp.where(dec_routes_ref[d, k] == here.e, dec_weight_ref[d, k], 0.0)
        dec_scale = jnp.where(row8 == d, one, dec_scale)

    def feed_forward(batch):
        places = BATCHES[batch]
        start, n = STARTS[batch], len(places)
        decode = batch == 2
        extra = 16 if decode else 0
        m, me = n * rows + extra, n * cap + extra
        lo = start * rows
        for j in range(n):
            at = lo + j * rows
            for half in range(2):
                xe[j * cap : (j + 1) * cap, half * hw : (half + 1) * hw] = nn(
                    pick[start + j], g[half, at : at + rows]
                ).astype(BF16)
        if decode:
            xe[n * cap : me] = dec_pad

        def up(i, carry):
            at = pl.multiple_of(i * 128, 128)
            w = jnp.concatenate([wgu[:, pl.ds(at, 128)], wgu[:, pl.ds(ff + at, 128)]], axis=1)
            hidden = nn(xe[0:me], w)
            he[0:me, pl.ds(at, 128)] = (silu(hidden[:, 0:128]) * hidden[:, 128:256]).astype(BF16)
            return carry

        lax.fori_loop(0, ff // 128, up, 0)

        scale = jnp.concatenate(
            [wslot[start + j][:, 0:1] for j in range(n)] + ([dec_scale] if decode else []), axis=0
        )

        def down(i, carry):
            cols = pl.ds(pl.multiple_of(i * tile, tile), tile)
            ye[0:me, cols] = (nn(he[0:me], wd[:, cols]) * scale).astype(BF16)
            return carry

        lax.fori_loop(0, width // tile, down, 0)

        for group in range(3):
            w = wsp.at[pl.ds(group * 256, 256)]
            hidden = nt(g[0, lo : lo + m], w[:, 0:hw]) + nt(g[1, lo : lo + m], w[:, hw:width])
            hs[0:m, group * 128 : (group + 1) * 128] = (
                silu(hidden[:, 0:128]) * hidden[:, 128:256]
            ).astype(BF16)
            if group == 2:
                logit = hidden[:, tail : tail + 1] + hidden[:, tail + 1 : tail + 2]
                gv[0:m] = jnp.broadcast_to(1.0 / (1.0 + jnp.exp(-logit)), (m, 128))

        for half in range(2):

            def combine(i, carry, half=half):
                here_cols = pl.ds(pl.multiple_of(i * tile, tile), tile)
                cols = pl.ds(pl.multiple_of(half * hw + i * tile, tile), tile)
                shared = nn(hs[0:m], wsd[:, cols]) * gv[0:m, 0:1]
                for j in range(n):
                    routed = nn(back[start + j][:, 0:cap], ye[j * cap : (j + 1) * cap, cols])
                    part[half, start + j, :, here_cols] = (
                        shared[j * rows : (j + 1) * rows] + routed
                    ).astype(BF16)
                if decode:
                    dec_send[2, :, cols] = (
                        shared[n * rows : n * rows + 8] + ye[n * cap : n * cap + 16, cols].astype(F32)[0:8]
                    ).astype(BF16)
                return carry

            lax.fori_loop(0, hw // tile, combine, 0)

    gather.to_batch_0()
    feed_forward(0)
    gather.to_batch_1()
    feed_forward(1)
    second.send_far(0)
    gather.to_batch_2()
    second.pass_on(0)
    feed_forward(2)
    second.send_far(2, 1, 3)
    for copy in dec_copies[2]:
        copy.start()
    second.pass_on(2, 1, 3)
    dec_send[3] = dec_sum(2).astype(BF16)
    for copy in dec_copies[3]:
        copy.start()
    halves = second.finish()
    for half in range(2):
        cols = pl.ds(half * hw, hw)
        out_ref[:, cols] = (res[:, cols].astype(F32) + halves[half]).astype(BF16)
    dec_out_ref[...] = (dec8[...] + dec_sum(3)).astype(BF16)[0:count]
    gather.close()
    second.close()
    for copy in meta_z + meta_x + sum(dec_copies, []):
        copy.wait_send()


def per_device(
    prefill_rows,
    decode_rows,
    key_values,
    cache_length,
    attention_gain,
    feedforward_gain,
    query_key_value,
    out_projection,
    routes,
    route_weight,
    decode_routes,
    decode_weight,
    expert_gate_up,
    expert_down,
    shared_gate_up,
    shared_down,
    shared_gate,
):
    rows, width = prefill_rows.shape
    hw = width // 2
    tokens = rows * 16
    count, span = decode_rows.shape[0], key_values.shape[2]
    cap = 3 * rows * routes.shape[1] // 32
    ff = expert_down.shape[1]
    vmem = pl.BlockSpec(memory_space=pltpu.VMEM)
    smem = pl.BlockSpec(memory_space=pltpu.SMEM)
    hbm = pl.BlockSpec(memory_space=pl.ANY)
    most = max(len(b) for b in BATCHES)
    attended, decode_attended = pl.pallas_call(
        attention_kernel,
        out_shape=(
            jax.ShapeDtypeStruct((tokens, HEAD_DIM), BF16),
            jax.ShapeDtypeStruct((8, HEAD_DIM), BF16),
        ),
        in_specs=[vmem, vmem, hbm, smem, vmem, hbm],
        out_specs=(vmem, vmem),
        scratch_shapes=[
            pltpu.VMEM((2, tokens, hw), BF16),
            pltpu.VMEM((3, width, HEAD_DIM), BF16),
            pltpu.VMEM((2, count, span, HEAD_DIM), BF16),
            pltpu.VMEM((3, tokens, HEAD_DIM), BF16),
            pltpu.VMEM((8, width), F32),
            pltpu.VMEM((2, 24, HEAD_DIM), F32),
            pltpu.VMEM((4, 24, HEAD_DIM), F32),
            pltpu.SemaphoreType.DMA((44,)),
            pltpu.SemaphoreType.DMA((44,)),
            pltpu.SemaphoreType.DMA((2,)),
        ],
        compiler_params=pltpu.CompilerParams(
            collective_id=0, has_side_effects=True, vmem_limit_bytes=48 * 1024 * 1024
        ),
        name="attend",
    )(
        prefill_rows,
        decode_rows,
        key_values,
        cache_length,
        attention_gain.reshape(1, width),
        jnp.transpose(query_key_value, (1, 0, 2)),
    )
    return pl.pallas_call(
        layer_kernel,
        out_shape=(
            jax.ShapeDtypeStruct((rows, width), BF16),
            jax.ShapeDtypeStruct((count, width), BF16),
        ),
        in_specs=[vmem] * 8 + [smem] * 2 + [vmem] + [hbm] * 4,
        out_specs=(vmem, vmem),
        scratch_shapes=[
            pltpu.VMEM((2, tokens + 16, hw), BF16),
            pltpu.VMEM((2, 16, rows, hw), BF16),
            pltpu.VMEM((2, 5, 2, rows // 2, hw), BF16),
            pltpu.VMEM((2, 5, 2, rows, hw), BF16),
            pltpu.VMEM((width, 2 * ff), BF16),
            pltpu.VMEM((ff, width), BF16),
            pltpu.VMEM((768, width), BF16),
            pltpu.VMEM((384, width), BF16),
            pltpu.VMEM((most * cap + 16, width), BF16),
            pltpu.VMEM((most * cap + 16, ff), BF16),
            pltpu.VMEM((most * cap + 16, width), BF16),
            pltpu.VMEM((most * rows + 16, 384), BF16),
            pltpu.VMEM((most * rows + 16, 128), F32),
            pltpu.VMEM((16, cap, 128), F32),
            pltpu.VMEM((16, cap, rows), BF16),
            pltpu.VMEM((16, rows, rows), BF16),
            pltpu.VMEM((4, 4, 16, rows), BF16),
            pltpu.VMEM((8, width), F32),
            pltpu.VMEM((4, 8, width), BF16),
            pltpu.VMEM((4, 3, 8, width), BF16),
            pltpu.VMEM((rows, width), BF16),
            pltpu.SemaphoreType.DMA((138,)),
            pltpu.SemaphoreType.DMA((138,)),
            pltpu.SemaphoreType.DMA((9,)),
        ],
        compiler_params=pltpu.CompilerParams(
            collective_id=1, has_side_effects=True, vmem_limit_bytes=67043328
        ),
        name="layer",
    )(
        prefill_rows,
        decode_rows,
        attended,
        decode_attended,
        feedforward_gain.reshape(1, width),
        out_projection,
        routes.T,
        route_weight.T,
        decode_routes,
        decode_weight,
        shared_gate.reshape(1, width),
        expert_gate_up[0],
        expert_down[0],
        jnp.transpose(shared_gate_up, (1, 2, 0)),
        shared_down,
    )


def solution(mesh):
    return jax.shard_map(
        per_device,
        mesh=mesh,
        in_specs=(
            P(("blk", "expert"), None),
            P(),
            P(None, None, "blk", "expert"),
            P(),
            P(),
            P(),
            P(None, None, "expert"),
            P("expert", None),
            P(("blk", "expert"), None),
            P(("blk", "expert"), None),
            P(),
            P(),
            P("expert", None, None),
            P("expert", None, None),
            P(None, None, "expert"),
            P("expert", None),
            P(),
        ),
        out_specs=(P(("blk", "expert"), None), P()),
        check_vma=False,
    )
```

time: 591 us -> 225 us (0.38); the launches traced: 583 us -> 224 us
  waiting for transfers between devices: 229 us -> 0 us
  Pallas kernels: 0 us -> 215 us
  blocking collectives: 186 us -> 0 us
  matrix products: 75.3 us -> 0 us
  local copies, waits for them, and re-layouts: 41.8 us -> 9.09 us
  other arithmetic: 25.8 us -> 0 us
  between operations: 14.2 us -> 0.67 us
  starting transfers between devices: 10.9 us -> 0 us
    pallas_call x0 -> x2, Pallas kernels: none -> 215 us  [the longest x1 154 us: per_device(): pl.pallas_call(layer_kernel, out_shape=(jax.ShapeDtypeStruct((rows, width...]
    psum x3 -> x0, blocking collectives: 171 us -> none  [the longest x1 79.6 us: per_device(): lax.psum((decode_scale[:, None] * decode_expert.astype(jnp.float32)).asty...]
    all_gather x2 -> x0, waiting for transfers between devices: 143 us -> none  [the longest x1 72.9 us: per_device(): lax.all_gather(prefill_rows, 'expert', axis=0, tiled=True)]
    reduce_scatter x2 -> x0, waiting for transfers between devices: 85.5 us -> none  [the longest x1 85.5 us: per_device(): lax.psum_scatter(jnp.dot(attended, out_projection, preferred_element_type...]
    dot_general x18 -> x0, matrix products: 75.3 us -> none  [the longest x4 29.1 us: gated_hidden(): hidden = jnp.dot(normed, gate_up, preferred_element_type=jnp.float32)]
    reduce_sum x13 -> x0, other arithmetic: 18.2 us -> none  [the longest x4 6.79 us: rms_normed(): jnp.mean(values * values, axis=-1, keepdims=True) + eps_norm]
    pmax x1 -> x0, blocking collectives: 14.9 us -> none  [per_device(): global_max = lax.pmax(local_max, 'blk')]
    scatter x1 -> x0, local copies, waits for them, and re-layouts: 12.4 us -> none  [per_device(): outgoing = jnp.zeros((experts_total * capacity, model_width), jnp.bfloat1...]
  transfers between devices with their start and end apart: 6 -> 0, of which waited for: 3 -> 0; matrix products, arithmetic and copies ran while one was open for 14% -> 0% of each run, Pallas kernels for 0% -> 0%
where the time goes in v1:
time: 225 us; the launch traced here: 224 us
  Pallas kernels  215 us (96%)
  local copies, waits for them, and re-layouts  9.09 us (4%)
    pallas_call x1, Pallas kernels, per_device(): pl.pallas_call(layer_kernel, out_shape=(jax.ShapeDtypeStruct((rows, width...  154 us
    pallas_call x1, Pallas kernels, per_device(): pl.pallas_call(attention_kernel, out_shape=(jax.ShapeDtypeStruct((tokens,...  60.7 us
    unnamed x16, local copies, waits for them, and re-layouts  9.09 us

profile of v1, /device:TPU:0, one launch (start us, length us, event | category | flops | bytes accessed | tf_op | source)
XLA Modules:
  0.0 224.3 jit_solution(11101285193300718129)
XLA Ops:
  0.6 0.0 copy-start
  0.6 1.0 copy-done
  1.7 0.0 copy-start.1
  1.7 1.4 copy-done.1
  3.1 0.0 copy-start.3
  3.1 0.7 copy-done.3
  3.8 0.0 copy-start.4
  3.8 0.7 copy-done.4
  4.5 0.0 copy-start.6
  4.5 0.7 copy-done.6
  5.2 60.7 %attend.1 = (bf16[2048,128]{1,0:T(8,128)(2,1)S(1)}, bf16[8,128]{1,0:T(8,128)(2,1)S(1)}) custom-call(bf16[128,2048]{1,0:T(8,128)(2,1)S(1)} %copy-done, bf16[4,2048]{1,0:T(4,128)(2,1)S(1)} %copy-done.3, bf16[2,4,2048,128]{3,2,1,0:T(8,128)(2,1)} %cache_hbm.1, s32[4]{0:T(128)S(1)} %copy-done.6, f32[1,2048]{1,0:T(1,128)S(1)} %bitcast.10, ...), custom_call_target="tpu_custom_call" | custom-call | tf_op jit(solution)/shard_map/attend/pallas_call | solution.py:744
  65.9 0.0 copy-start.2
  65.9 0.8 copy-done.2
  66.7 0.0 copy-start.5
  66.7 0.6 copy-done.5
  67.3 153.8 %layer.1 = (bf16[128,2048]{1,0:T(8,128)(2,1)}, bf16[4,2048]{1,0:T(4,128)(2,1)}) custom-call(bf16[128,2048]{1,0:T(8,128)(2,1)} %rows_ref.3, bf16[4,2048]{1,0:T(4,128)(2,1)} %dec_ref.3, bf16[2048,128]{1,0:T(8,128)(2,1)} %copy-done.2, bf16[8,128]{1,0:T(8,128)(2,1)} %copy-done.5, f32[1,2048]{1,0:T(1,128)} %bitcast.14, bf16[128,2048]{1,0:T(8,128)(2,1)} %wo_ref.1, ...), custom_call_target="tpu_custom_call" | custom-call | tf_op jit(solution)/shard_map/layer/pallas_call | solution.py:776
  221.1 1.9 copy.21
  222.9 1.3 copy.22
Async XLA Ops:
  0.6 1.0 copy-start
  1.7 1.4 copy-start.1
  3.1 0.7 copy-start.3
  3.8 0.7 copy-start.4
  4.5 0.7 copy-start.6
  65.9 0.8 copy-start.2
  66.7 0.6 copy-start.5

commit v2 on v1

--- a/solution.py
+++ b/solution.py
@@ -21,6 +21,8 @@
 )
 SLOT = {place: at for at, place in enumerate(sum(BATCHES, ()))}
 STARTS = (0, 5, 11)
+PAIR_BATCHES = (((0, 0), (0, 1), (0, 3), (1, 0)), ((0, 2), (1, 1), (1, 3), (1, 2)))
+PAIR = {place: at for at, place in enumerate(sum(PAIR_BATCHES, ()))}
 
 
 def nn(a, b):
@@ -47,11 +49,17 @@
         self.x = self.e // 4
         self.z = self.e % 4
 
+        odd = self.x % 2
+        self.mate = lambda: self.at(1 + 2 * odd, 0)
+        self.other = lambda: self.at(3 - 2 * odd, 0)
+        self.odd = odd
+
     def at(self, dx, dz):
         return (self.b, ((self.x + dx) % 4) * 4 + (self.z + dz) % 4)
 
     def block(self, place):
-        return ((self.x + place[0]) % 4) * 4 + (self.z + place[1]) % 4
+        half = self.odd if place[0] == 0 else 1 - self.odd
+        return half * 4 + (self.z + place[1]) % 4
 
 
 def greet(peers):
@@ -152,6 +160,147 @@
         for c in self.copies:
             for copy in c.values():
                 copy.wait_send()
+
+
+class PairGather:
+    def __init__(self, here, rows_ref, rows, send, recv):
+        hr = rows // 2
+        self.c = c = {}
+        z_p, z_m, mate = here.at(0, 1), here.at(0, 3), here.mate()
+
+        def put(name, half, src, dst, lo, size, device):
+            c[name] = remote(
+                rows_ref.at[half, pl.ds(PAIR[src] * rows + lo, size)],
+                rows_ref.at[half, pl.ds(PAIR[dst] * rows + lo, size)],
+                send,
+                recv,
+                len(c),
+                device,
+            )
+
+        for half, a in ((0, 0), (1, 0), (1, 1)):
+            put(("+", half, a), half, (a, 0), (a, 3), 0, rows, z_p)
+            put(("-", half, a), half, (a, 0), (a, 1), 0, rows, z_m)
+            put(("f+", half, a), half, (a, 3), (a, 2), hr, hr, z_p)
+            put(("f-", half, a), half, (a, 1), (a, 2), 0, hr, z_m)
+        for q in (0, 1, 3, 2):
+            put(("m", 0, q), 0, (0, q), (1, q), 0, rows, mate)
+        put(("m", 1, 0), 1, (0, 0), (1, 0), 0, rows, mate)
+
+    def start(self, *names):
+        for name in names:
+            self.c[name].start()
+
+    def got(self, *names):
+        for name in names:
+            self.c[name].wait_recv()
+
+    def open(self):
+        self.start(("+", 0, 0), ("-", 0, 0), ("m", 1, 0), ("m", 0, 0), ("+", 1, 0), ("-", 1, 0))
+
+    def to_batch_0(self):
+        self.got(("+", 0, 0), ("-", 0, 0))
+        self.start(("f+", 0, 0), ("f-", 0, 0), ("m", 0, 1), ("m", 0, 3))
+        self.got(("m", 1, 0))
+        self.start(("+", 1, 1), ("-", 1, 1))
+        self.got(("+", 1, 0), ("-", 1, 0))
+        self.start(("f+", 1, 0), ("f-", 1, 0))
+        self.got(("m", 0, 0))
+
+    def relay(self):
+        self.got(("f+", 0, 0), ("f-", 0, 0))
+        self.start(("m", 0, 2))
+        self.got(("+", 1, 1), ("-", 1, 1))
+        self.start(("f+", 1, 1), ("f-", 1, 1))
+
+    def to_batch_1(self):
+        self.got(("m", 0, 1), ("m", 0, 3), ("m", 0, 2))
+        self.got(("f+", 1, 0), ("f-", 1, 0), ("f+", 1, 1), ("f-", 1, 1))
+
+    def close(self):
+        for copy in self.c.values():
+            copy.wait_send()
+
+
+class PairScatter:
+    def __init__(self, here, part_ref, fwd_ref, full_ref, send, recv):
+        self.part, self.fwd, self.full = part_ref, fwd_ref, full_ref
+        self.c = c = {}
+        rows = part_ref.shape[2]
+        hr = rows // 2
+        self.low, self.high = pl.ds(0, hr), pl.ds(hr, hr)
+        z_p, z_m, mate = here.at(0, 1), here.at(0, 3), here.mate()
+
+        def put(name, src, dst, device):
+            c[name] = remote(src, dst, send, recv, len(c), device)
+
+        for half, a, k in ((0, 0, 4), (1, 1, 1), (1, 0, 0)):
+            far, plus, minus = PAIR[a, 2], PAIR[a, 1], PAIR[a, 3]
+            put(("f+", half, a), part_ref.at[half, far, self.low], fwd_ref.at[half, k, 0], z_p)
+            put(("f-", half, a), part_ref.at[half, far, self.high], fwd_ref.at[half, k, 1], z_m)
+            put(("t+", half, a), part_ref.at[half, plus], full_ref.at[half, k, 0], z_p)
+            put(("t-", half, a), part_ref.at[half, minus], full_ref.at[half, k, 1], z_m)
+        for q in range(4):
+            put(("m", 0, q), part_ref.at[0, PAIR[1, q]], full_ref.at[0, q, 0], mate)
+        put(("m", 1, 0), part_ref.at[1, PAIR[1, 0]], full_ref.at[1, 4, 0], mate)
+        self.slots = {(0, 0): 4, (1, 1): 1, (1, 0): 0}
+
+    def start(self, *names):
+        for name in names:
+            self.c[name].start()
+
+    def far(self, half, a):
+        self.start(("f+", half, a), ("f-", half, a))
+
+    def pass_plus(self, half, a):
+        self.c["f+", half, a].wait_recv()
+        at, k = PAIR[a, 1], self.slots[half, a]
+        self.part[half, at, self.low] = (
+            self.part[half, at, self.low].astype(F32) + self.fwd[half, k, 0].astype(F32)
+        ).astype(BF16)
+        self.c["t+", half, a].start()
+
+    def pass_minus(self, half, a):
+        self.c["f-", half, a].wait_recv()
+        at, k = PAIR[a, 3], self.slots[half, a]
+        self.part[half, at, self.high] = (
+            self.part[half, at, self.high].astype(F32) + self.fwd[half, k, 1].astype(F32)
+        ).astype(BF16)
+        self.c["t-", half, a].start()
+
+    def ring(self, half, a):
+        self.c["t+", half, a].wait_recv()
+        self.c["t-", half, a].wait_recv()
+        k = self.slots[half, a]
+        return (
+            self.part[half, PAIR[a, 0]].astype(F32)
+            + self.full[half, k, 0].astype(F32)
+            + self.full[half, k, 1].astype(F32)
+        )
+
+    def meet(self, q):
+        self.c["m", 0, q].wait_recv()
+        at = PAIR[0, q]
+        self.part[0, at] = (self.part[0, at].astype(F32) + self.full[0, q, 0].astype(F32)).astype(BF16)
+
+    def finish(self):
+        self.meet(2)
+        self.far(0, 0)
+        self.meet(1)
+        self.pass_plus(0, 0)
+        self.meet(3)
+        self.pass_minus(0, 0)
+        self.part[1, PAIR[1, 0]] = self.ring(1, 1).astype(BF16)
+        self.start(("m", 1, 0))
+        self.meet(0)
+        right = self.ring(1, 0)
+        left = self.ring(0, 0)
+        self.c["m", 1, 0].wait_recv()
+        return [left, right + self.full[1, 4, 0].astype(F32)]
+
+    def close(self):
+        for copy in self.c.values():
+            copy.wait_send()
 
 
 class Scatter:
@@ -264,8 +413,10 @@
     length_ref,
     gain_ref,
     qkv_hbm,
+    wo_hbm,
     att_ref,
     dec_att_ref,
+    wo_ref,
     g,
     wqkv,
     cache,
@@ -282,28 +433,48 @@
     hw = width // 2
     blk_count = lax.axis_size("blk")
     score_scale = 1.0 / math.sqrt(HEAD_DIM)
-    w_copy = pltpu.make_async_copy(qkv_hbm, wqkv, local_sem.at[0])
+    w_copy = pltpu.make_async_copy(qkv_hbm, wqkv.at[0], local_sem.at[0])
+    o_copy = pltpu.make_async_copy(wo_hbm, wo_ref.at[pl.ds(0, HEAD_DIM)], local_sem.at[2])
     c_copy = pltpu.make_async_copy(cache_hbm, cache, local_sem.at[1])
     w_copy.start()
+    o_copy.start()
     c_copy.start()
     core, y = here.b % 2, here.b // 2
     blk_peers = []
     if blk_count > 1:
         blk_peers = [(here.b + 1 - 2 * core, here.e)]
         blk_peers += [(((y + k) % 4) * 2 + core, here.e) for k in (1, 3, 2)]
-    wait_all = greet([here.at(1, 0), here.at(3, 0), here.at(0, 1), here.at(0, 3)] + blk_peers)
+    wait_all = greet([here.mate(), here.other(), here.at(0, 1), here.at(0, 3)] + blk_peers)
     own = normed(rows_ref[...].astype(F32), gain_ref[...])
     g[0, 0:rows] = own[:, :hw]
     g[1, 0:rows] = own[:, hw:]
     wait_all()
-    gather = Gather(here, g, rows, send, recv, 0)
+    gather = PairGather(here, g, rows, send, recv)
     gather.open()
+    w_half = pl.ds(pl.multiple_of(core * hw, hw), hw)
+    o_at = HEAD_DIM + core * (HEAD_DIM // 2)
+    o_half = pl.ds(pl.multiple_of(o_at, HEAD_DIM // 2), HEAD_DIM // 2)
+    o_src = pl.ds(pl.multiple_of(core * (HEAD_DIM // 2), HEAD_DIM // 2), HEAD_DIM // 2)
+    fetch, share = [], []
+    if blk_count > 1:
+        for i, (src, dst) in enumerate(
+            ((qkv_hbm.at[:, w_half], wqkv.at[1, :, w_half]), (wo_hbm.at[o_src], wo_ref.at[o_half]))
+        ):
+            fetch.append(remote(src, dst, send, recv, 36 + i, here.other()))
+            share.append(remote(dst, dst, send, recv, 38 + i, blk_peers[0]))
+    else:
+        for i, (src, dst) in enumerate(
+            ((qkv_hbm, wqkv.at[1]), (wo_hbm, wo_ref.at[pl.ds(HEAD_DIM, HEAD_DIM)]))
+        ):
+            fetch.append(remote(src, dst, send, recv, 36 + i, here.other()))
+    for copy in fetch:
+        copy.start()
 
     dn = normed(padded_rows(dec_ref, dec8), gain_ref[...])
     w_copy.wait()
-    q8 = nn(dn, wqkv[0]).astype(BF16)
-    k8 = nn(dn, wqkv[1]).astype(BF16)
-    v8 = nn(dn, wqkv[2]).astype(BF16)
+    q8 = nn(dn, wqkv[0, 0]).astype(BF16)
+    k8 = nn(dn, wqkv[0, 1]).astype(BF16)
+    v8 = nn(dn, wqkv[0, 2]).astype(BF16)
     c_copy.wait()
     count = cache.shape[1]
     span = cache.shape[2]
@@ -351,29 +522,36 @@
     for copy in blk_copies[:1]:
         copy.start()
 
-    q_s, k_s, v_s = heads.at[0], heads.at[1], heads.at[2]
-
-    def project(batch):
-        lo, size = STARTS[batch] * rows, len(BATCHES[batch]) * rows
+    def project(batch, head):
+        n = len(PAIR_BATCHES[batch])
+        lo, size = batch * n * rows, n * rows
         left, right = g[0, lo : lo + size], g[1, lo : lo + size]
-        for which, ref in enumerate((q_s, k_s, v_s)):
-            out = (nn(left, wqkv[which, 0:hw]) + nn(right, wqkv[which, hw:width])).astype(BF16)
-            for j, place in enumerate(BATCHES[batch]):
+        for which in range(3):
+            w = wqkv.at[head, which]
+            out = (nn(left, w[0:hw]) + nn(right, w[hw:width])).astype(BF16)
+            for j, place in enumerate(PAIR_BATCHES[batch]):
                 at = pl.multiple_of(here.block(place) * rows, rows)
-                ref[pl.ds(at, rows)] = out[j * rows : (j + 1) * rows]
+                heads[head, which, pl.ds(at, rows)] = out[j * rows : (j + 1) * rows]
 
     gather.to_batch_0()
-    project(0)
-    gather.to_batch_1()
+    project(0, 0)
+    gather.relay()
+    for copy in fetch:
+        copy.wait_recv()
+    for copy in share:
+        copy.start()
     if blk_copies:
         blk_copies[0].wait_recv()
         mix, top, total = merge(mix, top, total, 0)
         pack(1, mix, top, total)
         for copy in blk_copies[1:]:
             copy.start()
-    project(1)
-    gather.to_batch_2()
-    project(2)
+    for copy in share:
+        copy.wait_recv()
+    project(0, 1)
+    gather.to_batch_1()
+    project(1, 0)
+    project(1, 1)
     for k, copy in enumerate(blk_copies[1:]):
         copy.wait_recv()
         mix, top, total = merge(mix, top, total, k + 1)
@@ -389,27 +567,30 @@
         jnp.int32, (step, step), 1
     )
 
-    def one_request(r, carry):
-        first = pl.multiple_of(r * REQUEST_LEN, REQUEST_LEN)
+    def one_head(head, carry):
+        lanes = pl.ds(pl.multiple_of(head * HEAD_DIM, HEAD_DIM), HEAD_DIM)
         for qb in range(REQUEST_LEN // step):
-            at = pl.multiple_of(first + qb * step, step)
-            q = q_s[pl.ds(at, step)]
-            s1 = jnp.where(diagonal, nt(q, k_s[pl.ds(at, step)]) * score_scale, -jnp.inf)
+            at = qb * step
+            q = heads[head, 0, at : at + step]
+            s1 = jnp.where(diagonal, nt(q, heads[head, 1, at : at + step]) * score_scale, -jnp.inf)
             top_q = jnp.max(s1, axis=-1, keepdims=True)
             if qb:
-                s0 = nt(q, k_s[pl.ds(first, qb * step)]) * score_scale
+                s0 = nt(q, heads[head, 1, 0:at]) * score_scale
                 top_q = jnp.maximum(top_q, jnp.max(s0, axis=-1, keepdims=True))
             p1 = jnp.exp(s1 - top_q)
             sum_q = jnp.sum(p1, axis=-1, keepdims=True)
-            out = nn(p1.astype(BF16), v_s[pl.ds(at, step)])
+            out = nn(p1.astype(BF16), heads[head, 2, at : at + step])
             if qb:
                 p0 = jnp.exp(s0 - top_q)
                 sum_q = sum_q + jnp.sum(p0, axis=-1, keepdims=True)
-                out = out + nn(p0.astype(BF16), v_s[pl.ds(first, qb * step)])
-            att_ref[pl.ds(at, step)] = (out / sum_q).astype(BF16)
+                out = out + nn(p0.astype(BF16), heads[head, 2, 0:at])
+            att_ref[at : at + step, lanes] = (out / sum_q).astype(BF16)
         return carry
 
-    lax.fori_loop(0, att_ref.shape[0] // REQUEST_LEN, one_request, 0)
+    lax.fori_loop(0, 2, one_head, 0)
+    o_copy.wait()
+    for copy in fetch + share:
+        copy.wait_send()
     gather.close()
     for copy in blk_copies:
         copy.wait_send()
@@ -493,10 +674,10 @@
         for place in places:
             at = pl.multiple_of(here.block(place) * rows, rows)
             term = nn(att_ref[pl.ds(at, rows)], wo_ref[...]).astype(BF16)
-            part[0, SLOT[place]] = term[:, :hw]
-            part[1, SLOT[place]] = term[:, hw:]
-
-    first = Scatter(here, part, fwd, full, send, recv, 0)
+            part[0, PAIR[place]] = term[:, :hw]
+            part[1, PAIR[place]] = term[:, hw:]
+
+    first = PairScatter(here, part, fwd, full, send, recv)
     gather = Gather(here, g, rows, send, recv, 40)
     second = Scatter(here, part, fwd, full, send, recv, 80)
 
@@ -519,23 +700,28 @@
         exchange(dec_send.at[k], dec_recv.at[k], 126 + 3 * k, 1 - k % 2) for k in range(4)
     ]
 
-    out_project((2, 2))
-    dec_term = nn(dec_att_ref[...], wo_ref[...])
+    out_project((1, 2))
+    dec_term = nn(dec_att_ref[...], wo_ref[0:HEAD_DIM])
     dec_send[0] = dec_term.astype(BF16)
     wait_all()
-    first.send_far(2)
+    first.start(("m", 0, 2))
+    first.far(1, 1)
     for copy in meta_z + dec_copies[0]:
         copy.start()
-    out_project((2, 1), (1, 2))
-    first.send_far(1)
-    out_project((2, 3), (3, 2))
-    first.send_far(3)
-    out_project((2, 0), (0, 2))
-    first.send_far(0)
-    out_project((1, 1), (3, 1), (1, 3), (3, 3))
-    first.pass_on(2)
-    out_project((1, 0), (3, 0), (0, 1), (0, 3), (0, 0))
-    first.pass_on(1)
+    out_project((1, 1))
+    first.start(("m", 0, 1))
+    out_project((0, 2))
+    first.far(1, 0)
+    out_project((1, 3))
+    first.start(("m", 0, 3))
+    first.pass_plus(1, 1)
+    first.pass_minus(1, 1)
+    out_project((1, 0))
+    first.start(("m", 0, 0))
+    out_project((0, 1), (0, 3))
+    first.pass_plus(1, 0)
+    first.pass_minus(1, 0)
+    out_project((0, 0))
 
     def dec_sum(k):
         total = dec_send[k].astype(F32)
@@ -552,7 +738,6 @@
     dec_send[1] = dec_sum(0).astype(BF16)
     for copy in dec_copies[1]:
         copy.start()
-    first.pass_on(3, 0)
 
     gate = gate_ref[...]
     gate_coarse = gate.astype(BF16).astype(F32)
@@ -741,28 +926,29 @@
     smem = pl.BlockSpec(memory_space=pltpu.SMEM)
     hbm = pl.BlockSpec(memory_space=pl.ANY)
     most = max(len(b) for b in BATCHES)
-    attended, decode_attended = pl.pallas_call(
+    attended, decode_attended, projection = pl.pallas_call(
         attention_kernel,
         out_shape=(
-            jax.ShapeDtypeStruct((tokens, HEAD_DIM), BF16),
+            jax.ShapeDtypeStruct((tokens // 2, 2 * HEAD_DIM), BF16),
             jax.ShapeDtypeStruct((8, HEAD_DIM), BF16),
+            jax.ShapeDtypeStruct((2 * HEAD_DIM, width), BF16),
         ),
-        in_specs=[vmem, vmem, hbm, smem, vmem, hbm],
-        out_specs=(vmem, vmem),
+        in_specs=[vmem, vmem, hbm, smem, vmem, hbm, hbm],
+        out_specs=(vmem, vmem, vmem),
         scratch_shapes=[
-            pltpu.VMEM((2, tokens, hw), BF16),
-            pltpu.VMEM((3, width, HEAD_DIM), BF16),
+            pltpu.VMEM((2, tokens // 2, hw), BF16),
+            pltpu.VMEM((2, 3, width, HEAD_DIM), BF16),
             pltpu.VMEM((2, count, span, HEAD_DIM), BF16),
-            pltpu.VMEM((3, tokens, HEAD_DIM), BF16),
+            pltpu.VMEM((2, 3, tokens // 2, HEAD_DIM), BF16),
             pltpu.VMEM((8, width), F32),
             pltpu.VMEM((2, 24, HEAD_DIM), F32),
             pltpu.VMEM((4, 24, HEAD_DIM), F32),
             pltpu.SemaphoreType.DMA((44,)),
             pltpu.SemaphoreType.DMA((44,)),
-            pltpu.SemaphoreType.DMA((2,)),
+            pltpu.SemaphoreType.DMA((3,)),
         ],
         compiler_params=pltpu.CompilerParams(
-            collective_id=0, has_side_effects=True, vmem_limit_bytes=48 * 1024 * 1024
+            collective_id=0, has_side_effects=True, vmem_limit_bytes=67043328
         ),
         name="attend",
     )(
@@ -772,6 +958,7 @@
         cache_length,
         attention_gain.reshape(1, width),
         jnp.transpose(query_key_value, (1, 0, 2)),
+        out_projection,
     )
     return pl.pallas_call(
         layer_kernel,
@@ -817,7 +1004,7 @@
         attended,
         decode_attended,
         feedforward_gain.reshape(1, width),
-        out_projection,
+        projection,
         routes.T,
         route_weight.T,
         decode_routes,

time: 225 us -> 202 us (0.90)
  Pallas kernels: 215 us -> 197 us
  local copies, waits for them, and re-layouts: 9.09 us -> 3.21 us
    pallas_call x1, Pallas kernels: 60.7 us -> 44.6 us  [per_device(): pl.pallas_call(attention_kernel, out_shape=(jax.ShapeDtypeStruct((tokens...]
    unnamed x16 -> x2, local copies, waits for them, and re-layouts: 9.09 us -> 3.21 us
where the time goes in v2:
time: 202 us; the launch traced here: 201 us
  Pallas kernels  197 us (98%)
  local copies, waits for them, and re-layouts  3.21 us (2%)
    pallas_call x1, Pallas kernels, per_device(): pl.pallas_call(layer_kernel, out_shape=(jax.ShapeDtypeStruct((rows, width...  153 us
    pallas_call x1, Pallas kernels, per_device(): pl.pallas_call(attention_kernel, out_shape=(jax.ShapeDtypeStruct((tokens...  44.6 us

profile of v2, /device:TPU:0, one launch (start us, length us, event | category | flops | bytes accessed | tf_op | source)
XLA Modules:
  0.0 201.3 jit_solution(11717658359090788450)
XLA Ops:
  0.6 44.6 %attend.1 = (bf16[1024,256]{1,0:T(8,128)(2,1)}, bf16[8,128]{1,0:T(8,128)(2,1)}, bf16[256,2048]{1,0:T(8,128)(2,1)}) custom-call(bf16[128,2048]{1,0:T(8,128)(2,1)} %rows_ref.3, bf16[4,2048]{1,0:T(4,128)(2,1)} %dec_ref.3, bf16[2,4,2048,128]{3,2,1,0:T(8,128)(2,1)} %cache_hbm.1, s32[4]{0:T(128)} %length_ref.1, f32[1,2048]{1,0:T(1,128)} %bitcast.13, ...), custom_call_target="tpu_custom_call" | custom-call | tf_op jit(solution)/shard_map/attend/pallas_call | solution.py:929
  45.2 152.9 %layer.1 = (bf16[128,2048]{1,0:T(8,128)(2,1)}, bf16[4,2048]{1,0:T(4,128)(2,1)}) custom-call(bf16[128,2048]{1,0:T(8,128)(2,1)} %rows_ref.3, bf16[4,2048]{1,0:T(4,128)(2,1)} %dec_ref.3, bf16[1024,256]{1,0:T(8,128)(2,1)} %get-tuple-element.5.att_ref, bf16[8,128]{1,0:T(8,128)(2,1)} %get-tuple-element.6.dec_att_ref, f32[1,2048]{1,0:T(1,128)} %bitcast.14, ...), custom_call_target="tpu_custom_call" | custom-call | tf_op jit(solution)/shard_map/layer/pallas_call | solution.py:963
  198.1 1.9 copy.21
  200.0 1.3 copy.22

commit v3 on v2

--- a/solution.py
+++ b/solution.py
@@ -17,10 +17,11 @@
 BATCHES = (
     ((0, 0), (0, 1), (0, 3), (1, 0), (3, 0)),
     ((1, 1), (1, 3), (3, 1), (3, 3), (2, 0), (0, 2)),
-    ((1, 2), (3, 2), (2, 1), (2, 3), (2, 2)),
+    ((1, 2), (2, 1)),
+    ((3, 2), (2, 3), (2, 2)),
 )
 SLOT = {place: at for at, place in enumerate(sum(BATCHES, ()))}
-STARTS = (0, 5, 11)
+STARTS = (0, 5, 11, 13)
 PAIR_BATCHES = (((0, 0), (0, 1), (0, 3), (1, 0)), ((0, 2), (1, 1), (1, 3), (1, 2)))
 PAIR = {place: at for at, place in enumerate(sum(PAIR_BATCHES, ()))}
 
@@ -153,7 +154,10 @@
     def to_batch_2(self):
         self.got(("j+", 2), ("j-", 2))
         self.start(("f+", 2), ("f-", 2))
-        for q in (1, 3, 2):
+        self.got(("f+", 1), ("f-", 1))
+
+    def to_batch_3(self):
+        for q in (3, 2):
             self.got(("f+", q), ("f-", q))
 
     def close(self):
@@ -407,7 +411,7 @@
 
 
 def attention_kernel(
-    rows_ref,
+    rows_hbm,
     dec_ref,
     cache_hbm,
     length_ref,
@@ -416,7 +420,8 @@
     wo_hbm,
     att_ref,
     dec_att_ref,
-    wo_ref,
+    other_wo,
+    rows_ref,
     g,
     wqkv,
     cache,
@@ -434,10 +439,10 @@
     blk_count = lax.axis_size("blk")
     score_scale = 1.0 / math.sqrt(HEAD_DIM)
     w_copy = pltpu.make_async_copy(qkv_hbm, wqkv.at[0], local_sem.at[0])
-    o_copy = pltpu.make_async_copy(wo_hbm, wo_ref.at[pl.ds(0, HEAD_DIM)], local_sem.at[2])
+    r_copy = pltpu.make_async_copy(rows_hbm, rows_ref, local_sem.at[2])
+    r_copy.start()
     c_copy = pltpu.make_async_copy(cache_hbm, cache, local_sem.at[1])
     w_copy.start()
-    o_copy.start()
     c_copy.start()
     core, y = here.b % 2, here.b // 2
     blk_peers = []
@@ -445,6 +450,7 @@
         blk_peers = [(here.b + 1 - 2 * core, here.e)]
         blk_peers += [(((y + k) % 4) * 2 + core, here.e) for k in (1, 3, 2)]
     wait_all = greet([here.mate(), here.other(), here.at(0, 1), here.at(0, 3)] + blk_peers)
+    r_copy.wait()
     own = normed(rows_ref[...].astype(F32), gain_ref[...])
     g[0, 0:rows] = own[:, :hw]
     g[1, 0:rows] = own[:, hw:]
@@ -452,19 +458,17 @@
     gather = PairGather(here, g, rows, send, recv)
     gather.open()
     w_half = pl.ds(pl.multiple_of(core * hw, hw), hw)
-    o_at = HEAD_DIM + core * (HEAD_DIM // 2)
-    o_half = pl.ds(pl.multiple_of(o_at, HEAD_DIM // 2), HEAD_DIM // 2)
-    o_src = pl.ds(pl.multiple_of(core * (HEAD_DIM // 2), HEAD_DIM // 2), HEAD_DIM // 2)
+    o_half = pl.ds(pl.multiple_of(core * (HEAD_DIM // 2), HEAD_DIM // 2), HEAD_DIM // 2)
     fetch, share = [], []
     if blk_count > 1:
         for i, (src, dst) in enumerate(
-            ((qkv_hbm.at[:, w_half], wqkv.at[1, :, w_half]), (wo_hbm.at[o_src], wo_ref.at[o_half]))
+            ((qkv_hbm.at[:, w_half], wqkv.at[1, :, w_half]), (wo_hbm.at[o_half], other_wo.at[o_half]))
         ):
             fetch.append(remote(src, dst, send, recv, 36 + i, here.other()))
             share.append(remote(dst, dst, send, recv, 38 + i, blk_peers[0]))
     else:
         for i, (src, dst) in enumerate(
-            ((qkv_hbm, wqkv.at[1]), (wo_hbm, wo_ref.at[pl.ds(HEAD_DIM, HEAD_DIM)]))
+            ((qkv_hbm, wqkv.at[1]), (wo_hbm, other_wo))
         ):
             fetch.append(remote(src, dst, send, recv, 36 + i, here.other()))
     for copy in fetch:
@@ -588,7 +592,6 @@
         return carry
 
     lax.fori_loop(0, 2, one_head, 0)
-    o_copy.wait()
     for copy in fetch + share:
         copy.wait_send()
     gather.close()
@@ -597,12 +600,13 @@
 
 
 def layer_kernel(
-    rows_ref,
+    rows_hbm,
     dec_ref,
-    att_ref,
+    att_hbm,
     dec_att_ref,
     gain_ref,
-    wo_ref,
+    own_wo,
+    other_wo,
     routes_ref,
     weight_ref,
     dec_routes_ref,
@@ -614,6 +618,9 @@
     wsd_hbm,
     out_ref,
     dec_out_ref,
+    rows_ref,
+    att_ref,
+    wo_ref,
     g,
     part,
     fwd,
@@ -640,6 +647,19 @@
     local_sem,
 ):
     here = Place()
+    early = [
+        pltpu.make_async_copy(a, b, local_sem.at[9 + i])
+        for i, (a, b) in enumerate(
+            (
+                (att_hbm, att_ref),
+                (own_wo, wo_ref.at[pl.ds(0, HEAD_DIM)]),
+                (other_wo, wo_ref.at[pl.ds(HEAD_DIM, HEAD_DIM)]),
+                (rows_hbm, rows_ref),
+            )
+        )
+    ]
+    for copy in early:
+        copy.start()
     rows, width = rows_ref.shape
     hw = width // 2
     cap = pick.shape[1]
@@ -659,8 +679,6 @@
                 )
             )
     local = [pltpu.make_async_copy(a, b, local_sem.at[i]) for i, (a, b) in enumerate(moves)]
-    for copy in local:
-        copy.start()
     peers = [here.at(1, 0), here.at(3, 0), here.at(0, 1), here.at(0, 3), here.at(2, 0), here.at(0, 2)]
     wait_all = greet(peers)
 
@@ -700,13 +718,15 @@
         exchange(dec_send.at[k], dec_recv.at[k], 126 + 3 * k, 1 - k % 2) for k in range(4)
     ]
 
+    for copy in early:
+        copy.wait()
     out_project((1, 2))
     dec_term = nn(dec_att_ref[...], wo_ref[0:HEAD_DIM])
     dec_send[0] = dec_term.astype(BF16)
     wait_all()
     first.start(("m", 0, 2))
     first.far(1, 1)
-    for copy in meta_z + dec_copies[0]:
+    for copy in meta_z + dec_copies[0] + local:
         copy.start()
     out_project((1, 1))
     first.start(("m", 0, 1))
@@ -809,7 +829,7 @@
     def feed_forward(batch):
         places = BATCHES[batch]
         start, n = STARTS[batch], len(places)
-        decode = batch == 2
+        decode = batch == 3
         extra = 16 if decode else 0
         m, me = n * rows + extra, n * cap + extra
         lo = start * rows
@@ -875,14 +895,18 @@
     feed_forward(0)
     gather.to_batch_1()
     feed_forward(1)
+    gather.to_batch_2()
     second.send_far(0)
-    gather.to_batch_2()
+    feed_forward(2)
+    second.send_far(1)
     second.pass_on(0)
-    feed_forward(2)
-    second.send_far(2, 1, 3)
+    gather.to_batch_3()
+    second.pass_on(1)
+    feed_forward(3)
+    second.send_far(2, 3)
     for copy in dec_copies[2]:
         copy.start()
-    second.pass_on(2, 1, 3)
+    second.pass_on(2, 3)
     dec_send[3] = dec_sum(2).astype(BF16)
     for copy in dec_copies[3]:
         copy.start()
@@ -895,6 +919,11 @@
     second.close()
     for copy in meta_z + meta_x + sum(dec_copies, []):
         copy.wait_send()
+
+
+def write_kernel(a_ref, b_ref, a_out, b_out):
+    a_out[...] = a_ref[...]
+    b_out[...] = b_ref[...]
 
 
 def per_device(
@@ -931,11 +960,12 @@
         out_shape=(
             jax.ShapeDtypeStruct((tokens // 2, 2 * HEAD_DIM), BF16),
             jax.ShapeDtypeStruct((8, HEAD_DIM), BF16),
-            jax.ShapeDtypeStruct((2 * HEAD_DIM, width), BF16),
+            jax.ShapeDtypeStruct((HEAD_DIM, width), BF16),
         ),
-        in_specs=[vmem, vmem, hbm, smem, vmem, hbm, hbm],
-        out_specs=(vmem, vmem, vmem),
+        in_specs=[hbm, vmem, hbm, smem, vmem, hbm, hbm],
+        out_specs=(vmem, vmem, hbm),
         scratch_shapes=[
+            pltpu.VMEM((rows, width), BF16),
             pltpu.VMEM((2, tokens // 2, hw), BF16),
             pltpu.VMEM((2, 3, width, HEAD_DIM), BF16),
             pltpu.VMEM((2, count, span, HEAD_DIM), BF16),
@@ -960,15 +990,18 @@
         jnp.transpose(query_key_value, (1, 0, 2)),
         out_projection,
     )
-    return pl.pallas_call(
+    results = pl.pallas_call(
         layer_kernel,
         out_shape=(
             jax.ShapeDtypeStruct((rows, width), BF16),
             jax.ShapeDtypeStruct((count, width), BF16),
         ),
-        in_specs=[vmem] * 8 + [smem] * 2 + [vmem] + [hbm] * 4,
+        in_specs=[hbm, vmem, hbm, vmem, vmem, hbm, hbm, vmem, vmem] + [smem] * 2 + [vmem] + [hbm] * 4,
         out_specs=(vmem, vmem),
         scratch_shapes=[
+            pltpu.VMEM((rows, width), BF16),
+            pltpu.VMEM((tokens // 2, 2 * HEAD_DIM), BF16),
+            pltpu.VMEM((2 * HEAD_DIM, width), BF16),
             pltpu.VMEM((2, tokens + 16, hw), BF16),
             pltpu.VMEM((2, 16, rows, hw), BF16),
             pltpu.VMEM((2, 5, 2, rows // 2, hw), BF16),
@@ -992,7 +1025,7 @@
             pltpu.VMEM((rows, width), BF16),
             pltpu.SemaphoreType.DMA((138,)),
             pltpu.SemaphoreType.DMA((138,)),
-            pltpu.SemaphoreType.DMA((9,)),
+            pltpu.SemaphoreType.DMA((13,)),
         ],
         compiler_params=pltpu.CompilerParams(
             collective_id=1, has_side_effects=True, vmem_limit_bytes=67043328
@@ -1004,6 +1037,7 @@
         attended,
         decode_attended,
         feedforward_gain.reshape(1, width),
+        out_projection,
         projection,
         routes.T,
         route_weight.T,
@@ -1015,6 +1049,13 @@
         jnp.transpose(shared_gate_up, (1, 2, 0)),
         shared_down,
     )
+    return pl.pallas_call(
+        write_kernel,
+        out_shape=tuple(jax.ShapeDtypeStruct(r.shape, r.dtype) for r in results),
+        in_specs=[vmem, vmem],
+        out_specs=(vmem, vmem),
+        name="write",
+    )(*results)
 
 
 def solution(mesh):

time: 202 us -> 196 us (0.970)
  local copies, waits for them, and re-layouts: 3.21 us -> 0 us
    pallas_call x1, Pallas kernels: 153 us -> 149 us  [per_device(): pl.pallas_call(layer_kernel, out_shape=(jax.ShapeDtypeStruct((rows, width...]
    unnamed x2 -> x0, local copies, waits for them, and re-layouts: 3.21 us -> none
where the time goes in v3:
time: 196 us
  Pallas kernels  195 us (99%)
    pallas_call x1, Pallas kernels, per_device(): pl.pallas_call(layer_kernel, out_shape=(jax.ShapeDtypeStruct((rows, width...  149 us
    pallas_call x1, Pallas kernels, per_device(): pl.pallas_call(attention_kernel, out_shape=(jax.ShapeDtypeStruct((tokens...  43.9 us

profile of v3, /device:TPU:0, one launch (start us, length us, event | category | flops | bytes accessed | tf_op | source)
XLA Modules:
  0.0 195.7 jit_solution(10675893458647191737)
XLA Ops:
  0.6 43.9 %attend.1 = (bf16[1024,256]{1,0:T(8,128)(2,1)}, bf16[8,128]{1,0:T(8,128)(2,1)}, bf16[128,2048]{1,0:T(8,128)(2,1)}) custom-call(bf16[128,2048]{1,0:T(8,128)(2,1)} %rows_hbm.3, bf16[4,2048]{1,0:T(4,128)(2,1)} %dec_ref.3, bf16[2,4,2048,128]{3,2,1,0:T(8,128)(2,1)} %cache_hbm.1, s32[4]{0:T(128)} %length_ref.1, f32[1,2048]{1,0:T(1,128)} %bitcast.13, ...), custom_call_target="tpu_custom_call" | custom-call | tf_op jit(solution)/shard_map/attend/pallas_call | solution.py:958
  44.5 149.3 %layer.1 = (bf16[128,2048]{1,0:T(8,128)(2,1)}, bf16[4,2048]{1,0:T(4,128)(2,1)}) custom-call(bf16[128,2048]{1,0:T(8,128)(2,1)} %rows_hbm.3, bf16[4,2048]{1,0:T(4,128)(2,1)} %dec_ref.3, bf16[1024,256]{1,0:T(8,128)(2,1)} %get-tuple-element.7.att_hbm, bf16[8,128]{1,0:T(8,128)(2,1)} %get-tuple-element.8.dec_att_ref, f32[1,2048]{1,0:T(1,128)} %bitcast.14, ...), custom_call_target="tpu_custom_call" | custom-call | tf_op jit(solution)/shard_map/layer/pallas_call | solution.py:993
  193.8 1.9 write.1

commit v4 on v3

--- a/solution.py
+++ b/solution.py
@@ -386,9 +386,10 @@
         for half in range(2):
             self.part[half, slot(half, 0, q)] = self.total(half, q).astype(BF16)
 
-    def finish(self):
+    def finish(self, between):
         self.line(2)
         self.send_far(4)
+        between()
         self.line(1)
         for half in range(2):
             self.pass_plus(half, 4)
@@ -724,9 +725,11 @@
     dec_term = nn(dec_att_ref[...], wo_ref[0:HEAD_DIM])
     dec_send[0] = dec_term.astype(BF16)
     wait_all()
+    for copy in meta_z + dec_copies[0]:
+        copy.start()
     first.start(("m", 0, 2))
     first.far(1, 1)
-    for copy in meta_z + dec_copies[0] + local:
+    for copy in local:
         copy.start()
     out_project((1, 1))
     first.start(("m", 0, 1))
@@ -759,50 +762,6 @@
     for copy in dec_copies[1]:
         copy.start()
 
-    gate = gate_ref[...]
-    gate_coarse = gate.astype(BF16).astype(F32)
-    for copy in local:
-        copy.wait()
-    pad = 128 - tail
-    row_at = lax.broadcasted_iota(jnp.int32, (pad, width), 0)
-    wsp[512 + tail : 640] = jnp.where(
-        row_at == 0, gate_coarse, jnp.where(row_at == 1, gate - gate_coarse, 0.0)
-    ).astype(BF16)
-    wsp[640 + tail : 768] = jnp.zeros((pad, width), BF16)
-    wsd[sff : wsd.shape[0]] = jnp.zeros((wsd.shape[0] - sff, width), BF16)
-
-    for copy in meta_x:
-        copy.wait_recv()
-    expert = here.e.astype(F32)
-    iota_r = lax.broadcasted_iota(jnp.int32, (rows, rows), 0)
-    iota_c = lax.broadcasted_iota(jnp.int32, (rows, rows), 1)
-    upper = (iota_r <= iota_c).astype(F32).astype(BF16)
-    eye = (iota_r == iota_c).astype(F32).astype(BF16)
-    iota_cap = lax.broadcasted_iota(jnp.int32, (cap, rows), 0).astype(F32)
-    iota_lane = iota_c.astype(F32)
-    for place, at in SLOT.items():
-        info = meta[place[0], place[1]].astype(F32)
-        match = info[0:4] == expert
-        chosen = jnp.sum(match.astype(F32), axis=0, keepdims=True)
-        scale = jnp.sum(jnp.where(match, info[4:8] + info[8:12], 0.0), axis=0, keepdims=True)
-        order = nn(jnp.broadcast_to(chosen, (8, rows)).astype(BF16), upper)[0:1] - 1.0
-        order = jnp.where(chosen > 0.0, order, -1.0)
-        choice = iota_cap == order
-        pick[at] = choice.astype(F32).astype(BF16)
-        wslot[at] = jnp.broadcast_to(
-            jnp.sum(jnp.where(choice, scale, 0.0), axis=1, keepdims=True), (cap, 128)
-        )
-        column = nt(eye, jnp.broadcast_to(order, (8, rows)).astype(BF16))[:, 0:1]
-        back[at] = (iota_lane == column).astype(F32).astype(BF16)
-
-    dec_res = (padded_rows(dec_ref, dec8) + dec_sum(1)).astype(BF16).astype(F32)
-    dec_two = normed(dec_res, gain_ref[...])
-    dec8[...] = dec_res
-    base_row = 16 * rows
-    dec_pad = jnp.concatenate([dec_two.astype(F32), jnp.zeros((8, width), F32)], axis=0).astype(BF16)
-    g[0, base_row : base_row + 16] = dec_pad[:, :hw]
-    g[1, base_row : base_row + 16] = dec_pad[:, hw:]
-
     halves = first.finish()
     sum_sq = jnp.zeros((rows, 1), F32)
     for half in range(2):
@@ -816,6 +775,54 @@
         cols = pl.ds(half * hw, hw)
         g[half, 0:rows] = (res[:, cols].astype(F32) * factor * gain_ref[:, cols]).astype(BF16)
     gather.open()
+
+    gate = gate_ref[...]
+    gate_coarse = gate.astype(BF16).astype(F32)
+    for copy in local:
+        copy.wait()
+    pad = 128 - tail
+    row_at = lax.broadcasted_iota(jnp.int32, (pad, width), 0)
+    wsp[512 + tail : 640] = jnp.where(
+        row_at == 0, gate_coarse, jnp.where(row_at == 1, gate - gate_coarse, 0.0)
+    ).astype(BF16)
+    wsp[640 + tail : 768] = jnp.zeros((pad, width), BF16)
+    wsd[sff : wsd.shape[0]] = jnp.zeros((wsd.shape[0] - sff, width), BF16)
+
+    for copy in meta_x:
+        copy.wait_recv()
+    expert = here.e.astype(F32)
+    iota_r = lax.broadcasted_iota(jnp.int32, (rows, rows), 0)
+    iota_c = lax.broadcasted_iota(jnp.int32, (rows, rows), 1)
+    upper = (iota_r <= iota_c).astype(F32).astype(BF16)
+    eye = (iota_r == iota_c).astype(F32).astype(BF16)
+    iota_cap = lax.broadcasted_iota(jnp.int32, (cap, rows), 0).astype(F32)
+    iota_lane = iota_c.astype(F32)
+    chosen, scales = [], []
+    for place in SLOT:
+        info = meta[place[0], place[1]].astype(F32)
+        match = info[0:4] == expert
+        chosen.append(jnp.sum(match.astype(F32), axis=0, keepdims=True))
+        scales.append(jnp.sum(jnp.where(match, info[4:8] + info[8:12], 0.0), axis=0, keepdims=True))
+    chosen = jnp.concatenate(chosen, axis=0)
+    order = nn(chosen.astype(BF16), upper) - 1.0
+    order = jnp.where(chosen > 0.0, order, -1.0)
+    columns = nt(eye, order.astype(BF16))
+    for at in range(16):
+        choice = iota_cap == order[at : at + 1]
+        pick[at] = choice.astype(F32).astype(BF16)
+        wslot[at] = jnp.broadcast_to(
+            jnp.sum(jnp.where(choice, scales[at], 0.0), axis=1, keepdims=True), (cap, 128)
+        )
+        back[at] = (iota_lane == columns[:, at : at + 1]).astype(F32).astype(BF16)
+
+    dec_res = (padded_rows(dec_ref, dec8) + dec_sum(1)).astype(BF16).astype(F32)
+    dec_two = normed(dec_res, gain_ref[...])
+    dec8[...] = dec_res
+    base_row = 16 * rows
+    dec_pad = jnp.concatenate([dec_two.astype(F32), jnp.zeros((8, width), F32)], axis=0).astype(BF16)
+    g[0, base_row : base_row + 16] = dec_pad[:, :hw]
+    g[1, base_row : base_row + 16] = dec_pad[:, hw:]
+
     first.close()
 
     row8 = lax.broadcasted_iota(jnp.int32, (16, 1), 0)
@@ -903,14 +910,17 @@
     gather.to_batch_3()
     second.pass_on(1)
     feed_forward(3)
-    second.send_far(2, 3)
     for copy in dec_copies[2]:
         copy.start()
+    second.send_far(2, 3)
     second.pass_on(2, 3)
-    dec_send[3] = dec_sum(2).astype(BF16)
-    for copy in dec_copies[3]:
-        copy.start()
-    halves = second.finish()
+
+    def decode_turn():
+        dec_send[3] = dec_sum(2).astype(BF16)
+        for copy in dec_copies[3]:
+            copy.start()
+
+    halves = second.finish(decode_turn)
     for half in range(2):
         cols = pl.ds(half * hw, hw)
         out_ref[:, cols] = (res[:, cols].astype(F32) + halves[half]).astype(BF16)

time: 196 us -> 191 us (0.974)
  Pallas kernels: 195 us -> 190 us
    pallas_call x1, Pallas kernels: 149 us -> 145 us  [per_device(): pl.pallas_call(layer_kernel, out_shape=(jax.ShapeDtypeStruct((rows, width...]
where the time goes in v4:
time: 191 us
  Pallas kernels  190 us (99%)
    pallas_call x1, Pallas kernels, per_device(): pl.pallas_call(layer_kernel, out_shape=(jax.ShapeDtypeStruct((rows, width...  145 us
    pallas_call x1, Pallas kernels, per_device(): pl.pallas_call(attention_kernel, out_shape=(jax.ShapeDtypeStruct((tokens...  43.9 us

profile of v4, /device:TPU:0, one launch (start us, length us, event | category | flops | bytes accessed | tf_op | source)
XLA Modules:
  0.0 191.1 jit_solution(3080885606344820068)
XLA Ops:
  0.6 43.9 %attend.1 = (bf16[1024,256]{1,0:T(8,128)(2,1)}, bf16[8,128]{1,0:T(8,128)(2,1)}, bf16[128,2048]{1,0:T(8,128)(2,1)}) custom-call(bf16[128,2048]{1,0:T(8,128)(2,1)} %rows_hbm.3, bf16[4,2048]{1,0:T(4,128)(2,1)} %dec_ref.3, bf16[2,4,2048,128]{3,2,1,0:T(8,128)(2,1)} %cache_hbm.1, s32[4]{0:T(128)} %length_ref.1, f32[1,2048]{1,0:T(1,128)} %bitcast.13, ...), custom_call_target="tpu_custom_call" | custom-call | tf_op jit(solution)/shard_map/attend/pallas_call | solution.py:968
  44.5 144.7 %layer.1 = (bf16[128,2048]{1,0:T(8,128)(2,1)}, bf16[4,2048]{1,0:T(4,128)(2,1)}) custom-call(bf16[128,2048]{1,0:T(8,128)(2,1)} %rows_hbm.3, bf16[4,2048]{1,0:T(4,128)(2,1)} %dec_ref.3, bf16[1024,256]{1,0:T(8,128)(2,1)} %get-tuple-element.7.att_hbm, bf16[8,128]{1,0:T(8,128)(2,1)} %get-tuple-element.8.dec_att_ref, f32[1,2048]{1,0:T(1,128)} %bitcast.14, ...), custom_call_target="tpu_custom_call" | custom-call | tf_op jit(solution)/shard_map/layer/pallas_call | solution.py:1003
  189.2 1.9 write.1
